TPU v7x, 32 devices: a whole 2x2x4 slice. The times are simulated.
32 devices in a mesh: pb: 8 (over z, y), ka: 4 (over x, core).
Axes of the slice: x: 2, y: 2, z: 4, core: 2. Of those that a mesh axis runs over, the one named last changes fastest.
Arguments:
- pair_trunk: bfloat16 [384, 384, 128], P('pb', 'ka'), may hold values from -40 to 40
- token_ids: int32 [3, 384], replicated, may hold values from 0 to 422, as said below
- w_rel: bfloat16 [139, 128], replicated, may hold values from -3.5 to 3.5
- cat_gain: float32 [256], replicated, may hold values from 0.1 to 1.9
- w_in: bfloat16 [256, 128], replicated, may hold values from -0.375 to 0.375
- trans_gain: float32 [2, 128], replicated, may hold values from 0.1 to 1.9
- trans_ab: bfloat16 [2, 128, 512], replicated, may hold values from -0.5 to 0.5
- trans_out: bfloat16 [2, 256, 128], replicated, may hold values from -0.375 to 0.375
- bias_gain: float32 [128], replicated, may hold values from 0.1 to 1.9
- w_bias: bfloat16 [128, 16], replicated, may hold values from -1.5 to 1.5
- normed: bfloat16 [8, 384, 768], P(None, 'pb', 'ka'), may hold values from -12 to 12
- w_proj: bfloat16 [4, 768, 768], P(None, None, 'ka'), may hold values from -1 to 1
- output_weight: bfloat16 [768, 768], P('ka'), may hold values from -0.21875 to 0.21875
Outputs:
- pair_cond: bfloat16 [384, 384, 128], P('pb', 'ka')
- update: bfloat16 [8, 384, 768], P(None, 'pb', 'ka')
Inputs may be any that keep to these rules, and one draw needn't show every extreme that they name: `token_ids`: row 0 is a token's residue number, row 1 its chain number, row 2 its entity number. Chain numbers start at 0 and never fall along the tokens; residue numbers never fall within a chain; all tokens of a chain share one entity. The last token's residue number is 422.
All inputs are finite; a program needn't handle non-finite values.
Results may differ from a plain program's by a relative error of at most 0.015.
The roundings to bfloat16 on the way count: a program that leaves them out, or rounds other values in their place, can miss the bound.
Values may be sent and summed in bfloat16 or wider, within the bound.
A program may use at most 64 MiB of HBM per device.

v0:
```python
import math

import jax
import jax.numpy as jnp
from jax import lax
from jax.sharding import PartitionSpec as P

HD = 48
RMAX = 32
SMAX = 2
REL = 139


EPS = 1e-05


def layer_norm(values, scaling):
    average = jnp.mean(values, axis=-1, keepdims=True)
    centered = values - average
    spread = jnp.mean(centered * centered, axis=-1, keepdims=True)
    return centered * lax.rsqrt(spread + EPS) * scaling


def relative_onehot(query_token_ids, key_ids, query_pos, key_pos):
    query_res = query_token_ids[0][:, None]
    key_res = key_ids[0][None, :]
    query_chain = query_token_ids[1][:, None]
    key_chain = key_ids[1][None, :]
    query_entity = query_token_ids[2][:, None]
    key_ent = key_ids[2][None, :]
    same_chain = query_chain == key_chain
    same_res = same_chain & (query_res == key_res)
    same_entity = query_entity == key_ent
    res_bins = 2 * RMAX + 2
    res_bin = jnp.where(same_chain, jnp.clip(query_res - key_res + RMAX, 0, 2 * RMAX), 2 * RMAX + 1)
    token_offset_bin = jnp.where(
        same_res, jnp.clip(query_pos[:, None] - key_pos[None, :] + RMAX, 0, 2 * RMAX), 2 * RMAX + 1
    )
    chain_offset_bin = jnp.where(
        same_entity, jnp.clip(query_chain - key_chain + SMAX, 0, 2 * SMAX), 2 * SMAX + 1
    )
    columns = jnp.arange(REL, dtype=jnp.int32)
    onehot = (columns == res_bin[..., None]) | (columns == (res_bins + token_offset_bin)[..., None])
    onehot = onehot | (columns == (2 * res_bins + chain_offset_bin)[..., None])
    onehot = onehot | (columns == REL - 1) & same_entity[..., None]
    return onehot.astype(jnp.bfloat16)


def condition_block(
    trunk_blk, onehot, w_rel, cat_gain, w_in, trans_gain, trans_ab, trans_out, bias_gain, w_bias
):
    half = trans_out.shape[1]
    relative = jnp.einsum("rkf,fc->rkc", onehot, w_rel, preferred_element_type=jnp.float32)
    joined = jnp.concatenate([trunk_blk.astype(jnp.float32), relative], axis=-1)
    normal_in = layer_norm(joined, cat_gain).astype(jnp.bfloat16)
    pair_state = jnp.einsum("rkf,fc->rkc", normal_in, w_in, preferred_element_type=jnp.float32)
    for layer_idx in range(2):
        normal_tr = layer_norm(pair_state, trans_gain[layer_idx]).astype(jnp.bfloat16)
        gate_up = jnp.einsum(
            "rkc,cf->rkf", normal_tr, trans_ab[layer_idx], preferred_element_type=jnp.float32
        )
        hidden = (jax.nn.silu(gate_up[..., :half]) * gate_up[..., half:]).astype(jnp.bfloat16)
        pair_state = pair_state + jnp.einsum(
            "rkf,fc->rkc", hidden, trans_out[layer_idx], preferred_element_type=jnp.float32
        )
    normal_b = layer_norm(pair_state, bias_gain).astype(jnp.bfloat16)
    bias_blk = jnp.einsum(
        "rkc,ch->hrk", normal_b, w_bias, preferred_element_type=jnp.float32
    ).astype(jnp.bfloat16)
    return (pair_state.astype(jnp.bfloat16), bias_blk)


def soft_weights(logits):
    row_max = jnp.max(logits, axis=-1, keepdims=True)
    expweights = jnp.exp(logits - row_max)
    return (expweights / jnp.sum(expweights, axis=-1, keepdims=True)).astype(jnp.bfloat16)


def shards(
    pair_trunk,
    token_ids,
    w_rel,
    cat_gain,
    w_in,
    trans_gain,
    trans_ab,
    trans_out,
    bias_gain,
    w_bias,
    normed,
    w_proj,
    output_weight,
):
    q_rows = pair_trunk.shape[0]
    k_rows = pair_trunk.shape[1]
    q_start = lax.axis_index("pb") * q_rows
    k_start = lax.axis_index("ka") * k_rows
    key_ids = lax.dynamic_slice_in_dim(token_ids, k_start, k_rows, 1)
    key_pos = k_start + jnp.arange(k_rows, dtype=jnp.int32)
    row_blk = 8

    def one_block(block_idx):
        begin_at = block_idx * row_blk
        trunk_blk = lax.dynamic_slice_in_dim(pair_trunk, begin_at, row_blk, 0)
        query_token_ids = lax.dynamic_slice_in_dim(token_ids, q_start + begin_at, row_blk, 1)
        query_pos = q_start + begin_at + jnp.arange(row_blk, dtype=jnp.int32)
        onehot = relative_onehot(query_token_ids, key_ids, query_pos, key_pos)
        return condition_block(
            trunk_blk,
            onehot,
            w_rel,
            cat_gain,
            w_in,
            trans_gain,
            trans_ab,
            trans_out,
            bias_gain,
            w_bias,
        )

    pair_blocks, bias_blocks = lax.map(one_block, jnp.arange(q_rows // row_blk, dtype=jnp.int32))
    pair_cond = pair_blocks.reshape(q_rows, k_rows, pair_blocks.shape[-1])
    bias_tile = jnp.transpose(bias_blocks, (1, 0, 2, 3)).reshape(
        bias_blocks.shape[1], q_rows, k_rows
    )
    samples = normed.shape[0]
    feat_local = normed.shape[2]
    heads_local = feat_local // HD
    scale_factor = 1.0 / math.sqrt(HD)
    projected = jnp.einsum(
        "sqf,pfe->psqe",
        lax.all_gather(normed, "ka", axis=2, tiled=True),
        w_proj,
        preferred_element_type=jnp.float32,
    )
    queries = projected[0].astype(jnp.bfloat16).reshape(samples, q_rows, heads_local, HD)
    kv_local = jnp.transpose(
        jnp.stack([projected[1], projected[2]], axis=1).astype(jnp.bfloat16), (0, 1, 3, 2)
    )
    bias_rows = lax.all_to_all(bias_tile, "ka", split_axis=0, concat_axis=2, tiled=True)
    kv_all = lax.all_gather(kv_local, "pb", axis=3, tiled=True)
    keys_all = kv_all[:, 0].reshape(samples, heads_local, HD, kv_all.shape[3])
    values_all = kv_all[:, 1].reshape(samples, heads_local, HD, kv_all.shape[3])
    logits = (
        jnp.einsum("sqhd,shdk->shqk", queries, keys_all, preferred_element_type=jnp.float32)
        * scale_factor
    )
    logits = logits + bias_rows[None].astype(jnp.float32)
    weights = soft_weights(logits)
    attended = jnp.einsum(
        "shqk,shdk->sqhd", weights, values_all, preferred_element_type=jnp.float32
    )
    gated_result = (
        attended.reshape(samples, q_rows, feat_local) * jax.nn.sigmoid(projected[3])
    ).astype(jnp.bfloat16)
    flat_gated = gated_result.reshape(samples * q_rows, feat_local)
    summed = lax.psum_scatter(
        jnp.einsum(
            "fe,nf->en", output_weight, flat_gated, preferred_element_type=jnp.float32
        ).astype(jnp.bfloat16),
        "ka",
        scatter_dimension=0,
        tiled=True,
    ).astype(jnp.float32)
    update = jnp.transpose(summed).reshape(samples, q_rows, feat_local).astype(jnp.bfloat16)
    return (pair_cond, update)


def solution(mesh):
    in_specs = (
        P("pb", "ka", None),
        P(),
        P(),
        P(),
        P(),
        P(),
        P(),
        P(),
        P(),
        P(),
        P(None, "pb", "ka"),
        P(None, None, "ka"),
        P("ka", None),
    )
    out_specs = (P("pb", "ka", None), P(None, "pb", "ka"))
    return jax.shard_map(shards, mesh=mesh, in_specs=in_specs, out_specs=out_specs, check_vma=False)
```

profile of v0, /device:TPU:1, one launch (start us, length us, event | category | flops | bytes accessed | tf_op | source)
XLA Modules:
  0.0 147.9 jit_solution(9345763957200801556)
XLA Ops:
  7.2 1.3 copy.25
  8.5 14.2 %all_gather.6 = bf16[8,48,768]{1,0,2:T(8,128)(2,1)S(1)} all-gather(bf16[8,48,192]{1,0,2:T(8,128)(2,1)S(1)} %copy.25), channel_id=1, replica_groups=mesh['pb'=8,'ka'=4] {'ka'}, dimensions={2}, use_global_device_ids=true | all-gather | bytes 737280 | tf_op jit(solution)/shard_map/all_gather | solution.py:132
  22.7 1.6 %copy.26 = bf16[8,48,768]{2,1,0:T(8,128)(2,1)} copy(bf16[8,48,768]{1,0,2:T(8,128)(2,1)S(1)} %all_gather.6) | data formatting | bytes 1179648 | tf_op jit(solution)/shard_map/all_gather | solution.py:132
  24.3 1.9 %fusion.70 = (bf16[4,8,48,192]{3,2,1,0:T(8,128)(2,1)S(1)}, f32[4,8,48,192]{3,2,1,0:T(8,128)S(1)}) fusion(bf16[8,48,768]{2,1,0:T(8,128)(2,1)} %copy.26, bf16[4,768,192]{1,2,0:T(8,128)(2,1)S(1)} %copy-done), kind=kOutput, calls=%fused_computation.118 | convolution fusion | flops 453279744 | bytes 3538944 | tf_op jit(solution)/shard_map/sqf,pfe->psqe/dot_general | solution.py:130
  27.0 0.8 maximum_bitcast_fusion
  28.0 60.4 %while.13 = (s32[]{:T(128)}, bf16[6,8,96,128]{3,2,1,0:T(8,128)(2,1)}, bf16[6,16,8,96]{3,1,2,0:T(8,128)(2,1)}, s32[6]{0:T(128)S(1)}, bf16[48,96,128]{2,1,0:T(8,12...) while((s32[]{:T(128)}, ...), condition=%wide.region_10.11_spmd.clone, body=%wide.region_0.10_spmd.clone.sunk | while | flops 390749440 | bytes 15165903 | solution.py:121
  29.6 0.8 fusion.90
  30.4 1.0 dynamic-slice_convert_fusion.2
  31.3 1.1 fusion.91
  35.5 1.0 bitcast_dynamic-update-slice_fusion.2
  37.1 1.0 fusion.96
  40.4 1.0 dynamic-slice_convert_fusion.2
  41.4 1.1 fusion.91
  45.5 1.0 bitcast_dynamic-update-slice_fusion.2
  47.2 1.0 fusion.96
  49.7 0.8 fusion.90
  50.5 1.0 dynamic-slice_convert_fusion.2
  51.4 1.1 fusion.91
  55.6 1.0 bitcast_dynamic-update-slice_fusion.2
  57.2 1.0 fusion.96
  59.8 0.8 fusion.90
  60.5 1.0 dynamic-slice_convert_fusion.2
  61.5 1.1 fusion.91
  65.7 1.0 bitcast_dynamic-update-slice_fusion.2
  67.3 1.0 fusion.96
  70.6 1.0 dynamic-slice_convert_fusion.2
  71.6 1.1 fusion.91
  75.7 1.0 bitcast_dynamic-update-slice_fusion.2
  77.4 1.0 fusion.96
  80.7 1.0 dynamic-slice_convert_fusion.2
  81.6 1.1 fusion.91
  85.8 1.0 bitcast_dynamic-update-slice_fusion.2
  87.4 1.0 fusion.96
  88.4 1.7 %copy.48 = bf16[16,6,8,96]{3,2,1,0:T(8,128)(2,1)} copy(bf16[16,6,8,96]{3,0,2,1:T(8,128)(2,1)} %bitcast.136) | data formatting | bytes 294912 | tf_op jit(solution)/shard_map/transpose | solution.py:123
  90.1 4.1 %all-to-all-start = ((bf16[16,48,96]{2,1,0:T(8,128)(2,1)}), bf16[16,48,96]{2,1,0:T(8,128)(2,1)}, u32[]{:S(2)}, u32[]{:S(2)}) async-start(bf16[16,48,96]{2,1,0:T(8,128)(2,1)} %bitcast.106), calls=%async_computation | async-start | bytes 393216 | tf_op jit(solution)/shard_map/all_to_all | solution.py:140
  94.4 1.0 convert_element_type.75
  95.3 0.9 copy.33
  96.2 2.2 %all-to-all-done = bf16[16,48,96]{2,1,0:T(8,128)(2,1)} async-done(((bf16[16,48,96]{2,1,0:T(8,128)(2,1)}), bf16[16,48,96]{2,1,0:T(8,128)(2,1)}, u32[]{:S(2)}, u32[]{:S(2)}) %all-to-all-start) | async-done | bytes 147488 | tf_op jit(solution)/shard_map/all_to_all | solution.py:140
  98.4 1.0 convert_bitcast_fusion
  99.7 0.9 reshape.365
  100.6 3.4 %fusion.68 = (bf16[8,1,192,384]{2,3,0,1:T(8,128)(2,1)S(1)}, bf16[8,1,192,384]{2,3,0,1:T(8,128)(2,1)}) fusion(bf16[8,2,192,384]{2,3,0,1:T(8,128)(2,1)} %all-gather.2.cloned.1.call-done), kind=kLoop, calls=%fused_computation.116 | loop fusion | bytes 4718592 | tf_op jit(solution)/shard_map/slice | solution.py:142
  103.9 2.5 %copy.27 = bf16[8,1,192,384]{3,2,0,1:T(8,128)(2,1)} copy(bf16[8,1,192,384]{2,3,0,1:T(8,128)(2,1)} %get-tuple-element.183) | data formatting | bytes 2359296 | tf_op jit(solution)/shard_map/slice | solution.py:143
  106.5 1.5 %copy.28 = bf16[8,1,192,384]{3,2,0,1:T(8,128)(2,1)} copy(bf16[8,1,192,384]{2,3,0,1:T(8,128)(2,1)S(1)} %get-tuple-element.182) | data formatting | bytes 2359296 | tf_op jit(solution)/shard_map/slice | solution.py:142
  108.0 3.7 %fusion.71 = (f32[8,4,48]{2,1,0:T(4,128)S(1)}, f32[8,4,48,384]{3,2,1,0:T(8,128)}) fusion(f32[4,48,384]{2,1,0:T(8,128)} %reshape.365, bf16[8,4,48,384]{3,2,1,0:T(8,128)(2,1)} %bitcast.135, bf16[8,48,4,48]{3,2,1,0:T(4,128)(2,1)S(1)} %copy-done.5), kind=kOutput, calls=%fused_computation.119 | convolution fusion | flops 58982784 | bytes 3987456 | tf_op jit(solution)/shard_map/sub | solution.py:75
  111.6 2.3 %convolution_bitcast_fusion.1 = f32[8,48,4,48]{1,3,2,0:T(8,128)S(1)} fusion(bf16[8,4,48,384]{3,2,1,0:T(8,128)(2,1)S(1)} %bitcast.134, f32[8,4,48,384]{3,2,1,0:T(8,128)} %get-tuple-element.190, f32[8,4,48]{2,1,0:T(4,128)S(1)} %get-tuple-element.189), kind=kOutput, calls=%fused_computation.93 | convolution fusion | flops 57802752 | bytes 3840000 | tf_op jit(solution)/shard_map/shqk,shdk->sqhd/dot_general | solution.py:150
  115.4 1.1 copy.35
  116.5 22.9 %reduce-scatter.4.cloned.1.call-done = bf16[192,384]{1,0:T(8,128)(2,1)} async-done(((bf16[768,384]{1,0:T(8,128)(2,1)}), bf16[192,384]{1,0:T(8,128)(2,1)}) %reduce-scatter.4.cloned.1.call-update) | async-done | bytes 147472
  139.3 1.7 %copy.36 = bf16[192,384]{0,1:T(8,128)(2,1)} copy(bf16[192,384]{1,0:T(8,128)(2,1)} %reduce-scatter.4.cloned.1.call-done) | data formatting | bytes 294912
  (220 shorter events, 31.7 us)
Async XLA Ops:
  7.2 17.2 %copy-start = (bf16[4,768,192]{1,2,0:T(8,128)(2,1)S(1)}, bf16[4,768,192]{1,2,0:T(8,128)(2,1)}, u32[]{:S(2)}) copy-start(bf16[4,768,192]{1,2,0:T(8,128)(2,1)} %param.26) | copy-start | bytes 3538948
  7.2 93.4 %all-gather.2.cloned.1.call-start = ((), (), s32[]{:S(2)}) async-start(), calls=%async_computation.2 | async-start | bytes 3538944 | tf_op jit(solution)/shard_map/all_gather | solution.py:141
  26.2 1.7 %copy-start.9 = (s32[3,384]{1,0:T(4,128)S(1)}, s32[3,384]{1,0:T(4,128)}, u32[]{:S(2)}) copy-start(s32[3,384]{1,0:T(4,128)} %param.16) | copy-start | bytes 13828
  26.2 1.8 %copy-start.1 = (bf16[2,128,512]{2,1,0:T(8,128)(2,1)S(1)}, bf16[2,128,512]{2,1,0:T(8,128)(2,1)}, u32[]{:S(2)}) copy-start(bf16[2,128,512]{2,1,0:T(8,128)(2,1)} %param.21) | copy-start | bytes 786436
  26.2 1.8 %copy-start.7 = (bf16[128,16]{0,1:T(8,128)(2,1)S(1)}, bf16[128,16]{0,1:T(8,128)(2,1)}, u32[]{:S(2)}) copy-start(bf16[128,16]{0,1:T(8,128)(2,1)} %param.24) | copy-start | bytes 12292
  26.2 1.8 %copy-start.8 = (f32[2,128]{1,0:T(2,128)S(1)}, f32[2,128]{1,0:T(2,128)}, u32[]{:S(2)}) copy-start(f32[2,128]{1,0:T(2,128)} %param.20) | copy-start | bytes 3076
  26.2 1.7 %copy-start.10 = (f32[128]{0:T(128)S(1)}, f32[128]{0:T(128)}, u32[]{:S(2)}) copy-start(f32[128]{0:T(128)} %param.23) | copy-start | bytes 1540
  26.3 1.7 %copy-start.12 = (bf16[256,128]{1,0:T(8,128)(2,1)S(1)}, bf16[256,128]{1,0:T(8,128)(2,1)}, u32[]{:S(2)}) copy-start(bf16[256,128]{1,0:T(8,128)(2,1)} %param.19) | copy-start | bytes 196612
  26.3 1.7 %copy-start.13 = (bf16[139,128]{1,0:T(8,128)(2,1)S(1)}, bf16[139,128]{1,0:T(8,128)(2,1)}, u32[]{:S(2)}) copy-start(bf16[139,128]{1,0:T(8,128)(2,1)} %param.17) | copy-start | bytes 106756
  26.3 1.7 %copy-start.14 = (f32[256]{0:T(256)S(1)}, f32[256]{0:T(256)}, u32[]{:S(2)}) copy-start(f32[256]{0:T(256)} %param.18) | copy-start | bytes 3076
  33.3 0.9 copy-start.11
  43.4 0.9 copy-start.11
  53.5 0.9 copy-start.11
  63.5 0.9 copy-start.11
  73.6 0.9 copy-start.11
  83.7 0.9 copy-start.11
  88.4 5.9 %copy-start.4 = (bf16[1,8,48,192]{3,2,1,0:T(8,128)(2,1)S(1)}, bf16[1,8,48,192]{3,2,1,0:T(8,128)(2,1)}, u32[]{:S(2)}) copy-start(bf16[1,8,48,192]{3,2,1,0:T(8,128)(2,1)} %get-tuple-element.184) | copy-start | bytes 442372
  90.1 8.3 %all-to-all-start = ((bf16[16,48,96]{2,1,0:T(8,128)(2,1)}), bf16[16,48,96]{2,1,0:T(8,128)(2,1)}, u32[]{:S(2)}, u32[]{:S(2)}) async-start(bf16[16,48,96]{2,1,0:T(8,128)(2,1)} %bitcast.106), calls=%async_computation | async-start | bytes 393216 | tf_op jit(solution)/shard_map/all_to_all | solution.py:140
  94.2 45.1 %reduce-scatter.4.cloned.1.call-start = ((), (), s32[]{:S(2)}) async-start(), calls=%async_computation.3 | async-start | bytes 737280
  106.5 1.5 %copy-start.5 = (bf16[8,48,4,48]{3,2,1,0:T(4,128)(2,1)S(1)}, bf16[8,48,4,48]{3,2,1,0:T(4,128)(2,1)}, u32[]{:S(2)}) copy-start(bf16[8,48,4,48]{3,2,1,0:T(4,128)(2,1)} %convert_element_type.75) | copy-start | bytes 442372
  108.0 3.7 %copy-start.2 = (bf16[8,1,192,384]{3,2,0,1:T(8,128)(2,1)S(1)}, bf16[8,1,192,384]{3,2,0,1:T(8,128)(2,1)}, u32[]{:S(2)}) copy-start(bf16[8,1,192,384]{3,2,0,1:T(8,128)(2,1)} %copy.27) | copy-start | bytes 3538948
  113.9 1.0 copy-start.3
  113.9 1.1 copy-start.6
Sparse Core Ops, SparseCore 0:
  28.0 58.6 all-gather.1
  116.6 22.7 reduce-scatter.3
where the time goes:
time: 150 us; the launch traced here: 148 us
  matrix products  36.1 us (24%)
  waiting for transfers between devices  25.1 us (17%)
  other arithmetic  24.9 us (17%)
  local copies, waits for them, and re-layouts  24.6 us (16%)
  between operations  14.3 us (10%)
  blocking collectives  14.2 us (9%)
  loops' own time  4.59 us (3%)
  starting transfers between devices  4.13 us (3%)
    unnamed x3, waiting for transfers between devices  22.9 us
    all_gather x1, blocking collectives, shards(): lax.all_gather(normed, 'ka', axis=2, tiled=True)  14.2 us
    dot_general x12, matrix products, condition_block(): jnp.einsum('rkf,fc->rkc', hidden, trans_out[layer_idx], preferred_element...  8.84 us
    reduce_sum x24, other arithmetic, layer_norm(): spread = jnp.mean(centered * centered, axis=-1, keepdims=True)  8.35 us
    reduce_sum x12, other arithmetic, layer_norm(): average = jnp.mean(values, axis=-1, keepdims=True)  7.67 us
    dot_general x6, matrix products, condition_block(): jnp.einsum('rkc,ch->hrk', normal_b, w_bias, preferred_element_type=jnp.fl...  6.08 us
    convert_element_type x6, other arithmetic, condition_block(): joined = jnp.concatenate([trunk_blk.astype(jnp.float32), relative], axis=-1)  5.75 us
    dot_general x12, matrix products, condition_block(): jnp.einsum('rkc,cf->rkf', normal_tr, trans_ab[layer_idx], preferred_eleme...  5.06 us
  transfers between devices with their start and end apart: 3, of which 2 were waited for; matrix products, arithmetic and copies ran while one was open for 41% of the time, Pallas kernels for 0%

commit v1 on v0

v1 whole, which is shorter than its diff:
```python
import math
import functools

import jax
import jax.numpy as jnp
from jax import lax
from jax.experimental import pallas as pl
from jax.experimental.pallas import tpu as pltpu
from jax.sharding import PartitionSpec as P

HD = 48
RMAX = 32
SMAX = 2
REL = 139
EPS = 1e-05
F32 = jnp.float32
BF16 = jnp.bfloat16
ROWS = 16


def dot(a, b):
    return jnp.dot(a, b, preferred_element_type=F32)


def norm_rows(v, gain):
    centered = v - jnp.mean(v, axis=-1, keepdims=True)
    spread = jnp.mean(centered * centered, axis=-1, keepdims=True)
    return (centered * lax.rsqrt(spread + EPS) * gain).astype(BF16)


def onehot_row(q_res, q_chain, q_ent, q_pos, k_res, k_chain, k_ent, k_pos):
    shape = k_res.shape
    lane = lax.broadcasted_iota(jnp.int32, shape, 1)
    bins = 2 * RMAX + 2
    same_chain = k_chain == q_chain
    same_res = same_chain & (k_res == q_res)
    same_ent = k_ent == q_ent
    res_bin = jnp.where(same_chain, jnp.clip((q_res + RMAX) - k_res, 0, 2 * RMAX), bins - 1)
    tok_bin = jnp.where(
        same_res,
        jnp.clip((q_pos + (RMAX + bins)) - k_pos, bins, bins + 2 * RMAX),
        2 * bins - 1,
    )
    chain_bin = jnp.where(
        same_ent,
        jnp.clip((q_chain + (SMAX + 2 * bins)) - k_chain, 2 * bins, 2 * bins + 2 * SMAX),
        2 * bins + 2 * SMAX + 1,
    )
    low = (lane == res_bin) | (lane == tok_bin)
    high_lane = lane + 128
    high = (high_lane == tok_bin) | (high_lane == chain_bin)
    high = high | ((high_lane == REL - 1) & same_ent)
    one = jnp.where(low, 1.0, 0.0)
    two = jnp.where(high, 1.0, 0.0)
    return jnp.concatenate([one, two], axis=-1).astype(BF16)


def pair_block(
    begin,
    q_start,
    k_pos,
    tok_ref,
    key_ref,
    trunk_ref,
    wrel_scr,
    cat_gain_ref,
    w_in_ref,
    trans_gain_ref,
    ab_ref,
    out_ref,
    bias_gain_ref,
    w_bias_ref,
    pair_ref,
    bias_scr,
    bias_ref,
):
    keys = trunk_ref.shape[1]
    c = trunk_ref.shape[2]
    k_res, k_chain, k_ent = key_ref[0], key_ref[1], key_ref[2]
    rows = []
    for r in range(ROWS):
        at = q_start + begin + r
        rows.append(
            onehot_row(
                tok_ref[0, at], tok_ref[1, at], tok_ref[2, at], at, k_res, k_chain, k_ent, k_pos
            )
        )
    onehot = jnp.concatenate(rows, axis=0)
    rel = dot(onehot, wrel_scr[...])
    trunk = trunk_ref[pl.ds(begin, ROWS)].reshape(ROWS * keys, c).astype(F32)
    mean = jnp.sum(trunk + rel, axis=-1, keepdims=True) * (1.0 / (2 * c))
    ct = trunk - mean
    cr = rel - mean
    var = jnp.sum(ct * ct + cr * cr, axis=-1, keepdims=True) * (1.0 / (2 * c))
    inv = lax.rsqrt(var + EPS)
    gain = cat_gain_ref[...]
    normal_in = jnp.concatenate(
        [(ct * inv * gain[:, :c]).astype(BF16), (cr * inv * gain[:, c:]).astype(BF16)], axis=-1
    )
    state = dot(normal_in, w_in_ref[...])
    half = out_ref.shape[1]
    for l in range(2):
        normal = norm_rows(state, trans_gain_ref[l : l + 1, :])
        gate_up = dot(normal, ab_ref[l])
        gate_half = gate_up[:, :half] * 0.5
        silu = gate_half + gate_half * jnp.tanh(gate_half)
        hidden = (silu * gate_up[:, half:]).astype(BF16)
        state = state + dot(hidden, out_ref[l])
    pair_ref[pl.ds(begin, ROWS)] = state.astype(BF16).reshape(ROWS, keys, c)
    normal_b = norm_rows(state, bias_gain_ref[...])
    for r in range(ROWS):
        bias_scr[:, r, :] = lax.dot_general(
            w_bias_ref[...],
            normal_b[r * keys : (r + 1) * keys],
            (((0,), (1,)), ((), ())),
            preferred_element_type=F32,
        )
    bias_ref[:, pl.ds(begin, ROWS), :] = bias_scr[...].astype(BF16)


def pair_kernel(
    tok_ref, key_ref, trunk_ref, w_rel_ref, cat_gain_ref, w_in_ref, trans_gain_ref, ab_ref,
    out_ref, bias_gain_ref, w_bias_ref, pair_ref, bias_ref, wrel_scr, bias_scr,
):
    q_rows, keys = trunk_ref.shape[0], trunk_ref.shape[1]
    q_start = lax.axis_index("pb") * q_rows
    k_start = lax.axis_index("ka") * keys
    wrel_scr[...] = jnp.zeros_like(wrel_scr)
    wrel_scr[0:REL, :] = w_rel_ref[...]
    k_pos = k_start + lax.broadcasted_iota(jnp.int32, key_ref.shape[1:], 0)

    def step(i, carry):
        pair_block(
            pl.multiple_of(i * ROWS, ROWS), q_start, k_pos, tok_ref, key_ref, trunk_ref, wrel_scr,
            cat_gain_ref, w_in_ref, trans_gain_ref, ab_ref, out_ref, bias_gain_ref, w_bias_ref,
            pair_ref, bias_scr, bias_ref,
        )
        return carry

    lax.fori_loop(0, q_rows // ROWS, step, 0)


def pair_call(token_ids, key_cols, trunk, w_rel, cat_gain, w_in, trans_gain, ab, out, bias_gain, w_bias):
    q_rows, keys, c = trunk.shape
    heads = w_bias.shape[1]
    vmem = pl.BlockSpec(memory_space=pltpu.VMEM)
    return pl.pallas_call(
        pair_kernel,
        out_shape=(
            jax.ShapeDtypeStruct((q_rows, keys, c), BF16),
            jax.ShapeDtypeStruct((heads, q_rows, keys), BF16),
        ),
        in_specs=[pl.BlockSpec(memory_space=pltpu.SMEM)] + [vmem] * 10,
        out_specs=(vmem, vmem),
        scratch_shapes=[pltpu.VMEM((256, c), BF16), pltpu.VMEM((heads, ROWS, keys), F32)],
        compiler_params=pltpu.CompilerParams(vmem_limit_bytes=40 << 20),
        cost_estimate=pl.CostEstimate(flops=2300000000, bytes_accessed=4000000, transcendentals=0),
    )(token_ids, key_cols, trunk, w_rel, cat_gain.reshape(1, -1), w_in, trans_gain, ab, out,
      bias_gain.reshape(1, -1), w_bias)


def soft_weights(logits):
    row_max = jnp.max(logits, axis=-1, keepdims=True)
    expweights = jnp.exp(logits - row_max)
    return (expweights / jnp.sum(expweights, axis=-1, keepdims=True)).astype(jnp.bfloat16)


def shards(
    pair_trunk,
    token_ids,
    w_rel,
    cat_gain,
    w_in,
    trans_gain,
    trans_ab,
    trans_out,
    bias_gain,
    w_bias,
    normed,
    w_proj,
    output_weight,
):
    q_rows = pair_trunk.shape[0]
    k_rows = pair_trunk.shape[1]
    k_start = lax.axis_index("ka") * k_rows
    key_ids = lax.dynamic_slice_in_dim(token_ids, k_start, k_rows, 1)
    key_cols = jnp.broadcast_to(key_ids[:, :, None], (3, k_rows, 128))
    pair_cond, bias_tile = pair_call(
        token_ids, key_cols, pair_trunk, w_rel, cat_gain, w_in, trans_gain, trans_ab, trans_out,
        bias_gain, w_bias,
    )
    samples = normed.shape[0]
    feat_local = normed.shape[2]
    heads_local = feat_local // HD
    scale_factor = 1.0 / math.sqrt(HD)
    projected = jnp.einsum(
        "sqf,pfe->psqe",
        lax.all_gather(normed, "ka", axis=2, tiled=True),
        w_proj,
        preferred_element_type=jnp.float32,
    )
    queries = projected[0].astype(jnp.bfloat16).reshape(samples, q_rows, heads_local, HD)
    kv_local = jnp.transpose(
        jnp.stack([projected[1], projected[2]], axis=1).astype(jnp.bfloat16), (0, 1, 3, 2)
    )
    bias_rows = lax.all_to_all(bias_tile, "ka", split_axis=0, concat_axis=2, tiled=True)
    kv_all = lax.all_gather(kv_local, "pb", axis=3, tiled=True)
    keys_all = kv_all[:, 0].reshape(samples, heads_local, HD, kv_all.shape[3])
    values_all = kv_all[:, 1].reshape(samples, heads_local, HD, kv_all.shape[3])
    logits = (
        jnp.einsum("sqhd,shdk->shqk", queries, keys_all, preferred_element_type=jnp.float32)
        * scale_factor
    )
    logits = logits + bias_rows[None].astype(jnp.float32)
    weights = soft_weights(logits)
    attended = jnp.einsum(
        "shqk,shdk->sqhd", weights, values_all, preferred_element_type=jnp.float32
    )
    gated_result = (
        attended.reshape(samples, q_rows, feat_local) * jax.nn.sigmoid(projected[3])
    ).astype(jnp.bfloat16)
    flat_gated = gated_result.reshape(samples * q_rows, feat_local)
    summed = lax.psum_scatter(
        jnp.einsum(
            "fe,nf->en", output_weight, flat_gated, preferred_element_type=jnp.float32
        ).astype(jnp.bfloat16),
        "ka",
        scatter_dimension=0,
        tiled=True,
    ).astype(jnp.float32)
    update = jnp.transpose(summed).reshape(samples, q_rows, feat_local).astype(jnp.bfloat16)
    return (pair_cond, update)


def solution(mesh):
    in_specs = (
        P("pb", "ka", None),
        P(),
        P(),
        P(),
        P(),
        P(),
        P(),
        P(),
        P(),
        P(),
        P(None, "pb", "ka"),
        P(None, None, "ka"),
        P("ka", None),
    )
    out_specs = (P("pb", "ka", None), P(None, "pb", "ka"))
    return jax.shard_map(shards, mesh=mesh, in_specs=in_specs, out_specs=out_specs, check_vma=False)
```

time: 150 us -> 133 us (0.89)
  waiting for transfers between devices: 25.1 us -> 61.4 us
  matrix products: 36.1 us -> 8.23 us
  other arithmetic: 24.9 us -> 1.93 us
  Pallas kernels: 0 us -> 13.3 us
  local copies, waits for them, and re-layouts: 24.6 us -> 15.4 us
  loops' own time: 4.59 us -> 0 us
    all_gather x1, waiting for transfers between devices: 0.01 us -> 35.8 us  [shards(): kv_all = lax.all_gather(kv_local, 'pb', axis=3, tiled=True)]
    dot_general x42 -> x0, matrix products: 27.9 us -> none  [the longest x12 8.84 us: condition_block(): jnp.einsum('rkf,fc->rkc', hidden, trans_out[layer_idx], preferred_element...]
    reduce_sum x36 -> x0, other arithmetic: 16 us -> none  [the longest x24 8.35 us: layer_norm(): spread = jnp.mean(centered * centered, axis=-1, keepdims=True)]
    pallas_call x0 -> x1, Pallas kernels: none -> 13.3 us  [pair_call(): pl.pallas_call(pair_kernel, out_shape=(jax.ShapeDtypeStruct((q_rows, keys...]
    convert_element_type x7 -> x0, other arithmetic: 6.71 us -> none  [the longest x6 5.75 us: condition_block(): joined = jnp.concatenate([trunk_blk.astype(jnp.float32), relative], axis=-1)]
    another operation x1 -> x0, loops' own time: 4.59 us -> none  [shards(): lax.map(one_block, jnp.arange(q_rows // row_blk, dtype=jnp.int32))]
    dynamic_slice x12 -> x0, local copies, waits for them, and re-layouts: 4.28 us -> none  [the longest x6 3.82 us: shards(): lax.map(one_block, jnp.arange(q_rows // row_blk, dtype=jnp.int32))]
    transpose x1 -> x0, local copies, waits for them, and re-layouts: 1.69 us -> none  [shards(): jnp.transpose(bias_blocks, (1, 0, 2, 3))]
  transfers between devices with their start and end apart: 3 -> 3, of which waited for: 2 -> 3; matrix products, arithmetic and copies ran while one was open for 41% -> 2% of each run, Pallas kernels for 0% -> 10%
where the time goes in v1:
time: 133 us; the launch traced here: 132 us
  waiting for transfers between devices  61.4 us (46%)
  local copies, waits for them, and re-layouts  15.4 us (12%)
  blocking collectives  14.2 us (11%)
  between operations  14.2 us (11%)
  Pallas kernels  13.3 us (10%)
  matrix products  8.23 us (6%)
  starting transfers between devices  3.53 us (3%)
  other arithmetic  1.93 us (1%)
    all_gather x1, waiting for transfers between devices, shards(): kv_all = lax.all_gather(kv_local, 'pb', axis=3, tiled=True)  35.8 us
    unnamed x3, waiting for transfers between devices  22.5 us
    all_gather x1, blocking collectives, shards(): lax.all_gather(normed, 'ka', axis=2, tiled=True)  14.2 us
    pallas_call x1, Pallas kernels, pair_call(): pl.pallas_call(pair_kernel, out_shape=(jax.ShapeDtypeStruct((q_rows, keys...  13.3 us
    slice x2, local copies, waits for them, and re-layouts, shards(): keys_all = kv_all[:, 0].reshape(samples, heads_local, HD, kv_all.shape[3])  5.83 us
    unnamed x30, local copies, waits for them, and re-layouts  4.67 us
    sub x1, matrix products, soft_weights(): expweights = jnp.exp(logits - row_max)  3.64 us
    all_to_all x1, starting transfers between devices, shards(): lax.all_to_all(bias_tile, 'ka', split_axis=0, concat_axis=2, tiled=True)  3.49 us
  transfers between devices with their start and end apart: 3, of which 3 were waited for; matrix products, arithmetic and copies ran while one was open for 2% of the time, Pallas kernels for 10%

profile of v1, /device:TPU:1, one launch (start us, length us, event | category | flops | bytes accessed | tf_op | source)
XLA Modules:
  0.0 132.2 jit_solution(17913519714056721484)
XLA Ops:
  7.2 0.0 copy-start
  7.2 0.0 all-gather.2.cloned.1.call-start
  7.2 1.3 copy.27
  8.5 14.2 %all_gather.6 = bf16[8,48,768]{1,0,2:T(8,128)(2,1)S(1)} all-gather(bf16[8,48,192]{1,0,2:T(8,128)(2,1)S(1)} %copy.27), channel_id=1, replica_groups=mesh['pb'=8,'ka'=4] {'ka'}, dimensions={2}, use_global_device_ids=true | all-gather | bytes 737280 | tf_op jit(solution)/shard_map/all_gather | solution.py:198
  22.7 1.0 copy.28
  23.7 0.0 copy-done
  23.7 1.9 %fusion.21 = (bf16[4,8,48,192]{3,2,1,0:T(8,128)(2,1)S(1)}, f32[4,8,48,192]{3,2,1,0:T(8,128)}) fusion(bf16[8,48,768]{2,1,0:T(8,128)(2,1)S(1)} %copy.28, bf16[4,768,192]{1,2,0:T(8,128)(2,1)S(1)} %copy-done), kind=kOutput, calls=%fused_computation.28 | convolution fusion | flops 453279744 | bytes 3538944 | tf_op jit(solution)/shard_map/sqf,pfe->psqe/dot_general | solution.py:196
  25.7 0.0 copy-start.4
  25.7 0.0 copy-start.5
  25.7 0.0 copy-start.6
  25.7 0.0 copy-start.7
  25.7 0.0 copy-start.8
  25.7 0.0 copy-start.9
  25.8 0.8 maximum_bitcast_fusion
  26.6 0.0 all-gather.2.cloned.1.call-update
  26.6 0.0 copy-done.12
  26.6 0.1 copy.26.w_bias_ref
  26.8 0.0 copy-done.1
  26.8 0.1 constant_dynamic-slice_fusion
  26.9 0.1 broadcast_in_dim.2.key_ref
  27.0 0.1 copy-done.2
  27.1 0.0 copy-done.3
  27.1 0.0 copy-done.4
  27.2 0.0 copy-done.5
  27.2 0.0 copy-done.6
  27.2 13.3 %shard_map.140 = (bf16[48,96,128]{2,1,0:T(8,128)(2,1)}, bf16[16,48,96]{2,1,0:T(8,128)(2,1)}) custom-call(s32[3,384]{1,0:T(4,128)S(1)} %copy-done.1, s32[3,96,128]{2,1,0:T(8,128)S(1)} %broadcast_in_dim.2.key_ref, bf16[48,96,128]{2,1,0:T(8,128)(2,1)S(1)} %copy-done.2, bf16[139,128]{1,0:T(8,128)(2,1)S(1)} %copy-done.6, f32[1,256]{1,0:T(1,128)S(1)} %bitcast.47, ...), custom_call_target="tpu_custom_call" | custom-call | flops 2300000000 | bytes 4000000 | tf_op jit(solution)/shard_map/pallas_call | solution.py:147
  40.5 3.5 %all-to-all-start = ((bf16[16,48,96]{2,1,0:T(8,128)(2,1)}), bf16[16,48,96]{2,1,0:T(8,128)(2,1)S(1)}, u32[]{:S(2)}, u32[]{:S(2)}) async-start(bf16[16,48,96]{2,1,0:T(8,128)(2,1)} %get-tuple-element.5), calls=%async_computation | async-start | bytes 393216 | tf_op jit(solution)/shard_map/all_to_all | solution.py:206
  44.0 1.1 fusion.9
  45.1 0.2 convert_element_type.44
  45.3 0.1 copy.34
  45.4 3.0 %all-to-all-done = bf16[16,48,96]{2,1,0:T(8,128)(2,1)S(1)} async-done(((bf16[16,48,96]{2,1,0:T(8,128)(2,1)}), bf16[16,48,96]{2,1,0:T(8,128)(2,1)S(1)}, u32[]{:S(2)}, u32[]{:S(2)}) %all-to-all-start) | async-done | bytes 147488 | tf_op jit(solution)/shard_map/all_to_all | solution.py:206
  48.4 0.2 copy.49
  48.6 0.9 reshape.45
  49.5 35.8 %all-gather.2.cloned.1.call-done = bf16[8,2,192,384]{2,3,0,1:T(8,128)(2,1)} async-done(((bf16[8,2,192,48]{2,3,0,1:T(8,128)(2,1)}), bf16[8,2,192,384]{2,3,0,1:T(8,128)(2,1)}) %all-gather.2.cloned.1.call-update) | async-done | bytes 2359312 | tf_op jit(solution)/shard_map/all_gather | solution.py:207
  85.4 3.3 %fusion.19 = (bf16[8,1,192,384]{2,3,0,1:T(8,128)(2,1)}, bf16[8,1,192,384]{2,3,0,1:T(8,128)(2,1)S(1)}) fusion(bf16[8,2,192,384]{2,3,0,1:T(8,128)(2,1)} %all-gather.2.cloned.1.call-done), kind=kLoop, calls=%fused_computation.26 | loop fusion | bytes 4718592 | tf_op jit(solution)/shard_map/slice | solution.py:208
  88.7 2.5 %copy.30 = bf16[8,1,192,384]{3,2,0,1:T(8,128)(2,1)} copy(bf16[8,1,192,384]{2,3,0,1:T(8,128)(2,1)} %get-tuple-element.6) | data formatting | bytes 2359296 | tf_op jit(solution)/shard_map/slice | solution.py:208
  91.2 1.5 %copy.29 = bf16[8,1,192,384]{3,2,0,1:T(8,128)(2,1)} copy(bf16[8,1,192,384]{2,3,0,1:T(8,128)(2,1)S(1)} %get-tuple-element.7) | data formatting | bytes 2359296 | tf_op jit(solution)/shard_map/slice | solution.py:209
  92.7 3.6 %fusion.22 = (f32[8,4,48]{2,1,0:T(4,128)S(1)}, f32[8,4,48,384]{3,2,1,0:T(8,128)}) fusion(f32[4,48,384]{2,1,0:T(8,128)} %reshape.45, bf16[8,4,48,384]{3,2,1,0:T(8,128)(2,1)} %bitcast.51, bf16[8,48,4,48]{3,2,1,0:T(4,128)(2,1)S(1)} %convert_element_type.44), kind=kOutput, calls=%fused_computation.29 | convolution fusion | flops 58982784 | bytes 3987456 | tf_op jit(solution)/shard_map/sub | solution.py:164
  96.4 2.3 %convolution_bitcast_fusion.1 = f32[8,48,4,48]{1,3,2,0:T(8,128)S(1)} fusion(bf16[8,4,48,384]{3,2,1,0:T(8,128)(2,1)S(1)} %bitcast.52, f32[8,4,48,384]{3,2,1,0:T(8,128)} %get-tuple-element.14, f32[8,4,48]{2,1,0:T(4,128)S(1)} %get-tuple-element.13), kind=kOutput, calls=%fused_computation.7 | convolution fusion | flops 57802752 | bytes 3840000 | tf_op jit(solution)/shard_map/shqk,shdk->sqhd/dot_general | solution.py:216
  98.7 0.0 copy-start.11
  98.7 0.5 copy.33
  99.1 0.3 reshape.44
  99.4 0.2 copy-done.11
  99.6 0.4 fusion.2
  100.0 1.1 copy.36
  101.1 0.0 reduce-scatter.4.cloned.1.call-update
  101.1 22.5 %reduce-scatter.4.cloned.1.call-done = bf16[192,384]{1,0:T(8,128)(2,1)} async-done(((bf16[768,384]{1,0:T(8,128)(2,1)}), bf16[192,384]{1,0:T(8,128)(2,1)}) %reduce-scatter.4.cloned.1.call-update) | async-done | bytes 147472
  123.6 1.7 %copy.37 = bf16[192,384]{0,1:T(8,128)(2,1)} copy(bf16[192,384]{1,0:T(8,128)(2,1)} %reduce-scatter.4.cloned.1.call-done) | data formatting | bytes 294912
  (11 shorter events, 0.1 us)
Async XLA Ops:
  7.2 16.5 %copy-start = (bf16[4,768,192]{1,2,0:T(8,128)(2,1)S(1)}, bf16[4,768,192]{1,2,0:T(8,128)(2,1)}, u32[]{:S(2)}) copy-start(bf16[4,768,192]{1,2,0:T(8,128)(2,1)} %param.24) | copy-start | bytes 3538948
  7.2 78.2 %all-gather.2.cloned.1.call-start = ((), (), s32[]{:S(2)}) async-start(), calls=%async_computation.2 | async-start | bytes 3538944 | tf_op jit(solution)/shard_map/all_gather | solution.py:207
  25.6 1.0 copy-start.12
  25.7 1.1 copy-start.1
  25.7 1.4 %copy-start.2 = (bf16[48,96,128]{2,1,0:T(8,128)(2,1)S(1)}, bf16[48,96,128]{2,1,0:T(8,128)(2,1)}, u32[]{:S(2)}) copy-start(bf16[48,96,128]{2,1,0:T(8,128)(2,1)} %trunk_ref.1) | copy-start | bytes 3538948
  25.7 1.5 %copy-start.3 = (bf16[2,128,512]{2,1,0:T(8,128)(2,1)S(1)}, bf16[2,128,512]{2,1,0:T(8,128)(2,1)}, u32[]{:S(2)}) copy-start(bf16[2,128,512]{2,1,0:T(8,128)(2,1)} %ab_ref.1) | copy-start | bytes 786436
  25.7 1.5 %copy-start.4 = (bf16[2,256,128]{2,1,0:T(8,128)(2,1)S(1)}, bf16[2,256,128]{2,1,0:T(8,128)(2,1)}, u32[]{:S(2)}) copy-start(bf16[2,256,128]{2,1,0:T(8,128)(2,1)} %out_ref.1) | copy-start | bytes 393220
  25.7 1.5 %copy-start.5 = (bf16[256,128]{1,0:T(8,128)(2,1)S(1)}, bf16[256,128]{1,0:T(8,128)(2,1)}, u32[]{:S(2)}) copy-start(bf16[256,128]{1,0:T(8,128)(2,1)} %w_in_ref.1) | copy-start | bytes 196612
  25.7 1.5 %copy-start.6 = (bf16[139,128]{1,0:T(8,128)(2,1)S(1)}, bf16[139,128]{1,0:T(8,128)(2,1)}, u32[]{:S(2)}) copy-start(bf16[139,128]{1,0:T(8,128)(2,1)} %w_rel_ref.1) | copy-start | bytes 106756
  25.7 1.5 %copy-start.7 = (f32[256]{0:T(256)S(1)}, f32[256]{0:T(256)}, u32[]{:S(2)}) copy-start(f32[256]{0:T(256)} %param.16) | copy-start | bytes 3076
  25.7 1.5 %copy-start.8 = (f32[2,128]{1,0:T(2,128)S(1)}, f32[2,128]{1,0:T(2,128)}, u32[]{:S(2)}) copy-start(f32[2,128]{1,0:T(2,128)} %trans_gain_ref.1) | copy-start | bytes 3076
  25.7 1.5 %copy-start.9 = (f32[128]{0:T(128)S(1)}, f32[128]{0:T(128)}, u32[]{:S(2)}) copy-start(f32[128]{0:T(128)} %param.21) | copy-start | bytes 1540
  40.5 8.0 %all-to-all-start = ((bf16[16,48,96]{2,1,0:T(8,128)(2,1)}), bf16[16,48,96]{2,1,0:T(8,128)(2,1)S(1)}, u32[]{:S(2)}, u32[]{:S(2)}) async-start(bf16[16,48,96]{2,1,0:T(8,128)(2,1)} %get-tuple-element.5), calls=%async_computation | async-start | bytes 393216 | tf_op jit(solution)/shard_map/all_to_all | solution.py:206
  44.0 79.6 %reduce-scatter.4.cloned.1.call-start = ((), (), s32[]{:S(2)}) async-start(), calls=%async_computation.3 | async-start | bytes 737280
  92.7 3.6 %copy-start.10 = (bf16[8,1,192,384]{3,2,0,1:T(8,128)(2,1)S(1)}, bf16[8,1,192,384]{3,2,0,1:T(8,128)(2,1)}, u32[]{:S(2)}) copy-start(bf16[8,1,192,384]{3,2,0,1:T(8,128)(2,1)} %copy.29) | copy-start | bytes 3538948
  98.7 1.0 copy-start.11
Sparse Core Ops, SparseCore 0:
  26.8 58.5 all-gather.1
  101.2 22.3 reduce-scatter.3

commit v2 on v1

--- a/solution.py
+++ b/solution.py
@@ -118,45 +118,265 @@
     bias_ref[:, pl.ds(begin, ROWS), :] = bias_scr[...].astype(BF16)
 
 
+MESH = pl.DeviceIdType.MESH
+
+
+def ka_peer(offset):
+    size = lax.axis_size("ka")
+    return lax.rem(lax.axis_index("ka") + offset, size)
+
+
+def ring_index(pos):
+    n = lax.axis_size("pb")
+    pos = lax.rem(pos + 2 * n, n)
+    if n % 2:
+        return pos
+    return jnp.where(pos < n // 2, 2 * pos, 2 * (n - 1 - pos) + 1)
+
+
+def ring_position(index):
+    n = lax.axis_size("pb")
+    if n % 2:
+        return index
+    half = index // 2
+    return jnp.where(lax.rem(index, 2) == 0, half, n - 1 - half)
+
+
+def gather_kernel(x_ref, o_ref, local_sem, send_sem, recv_sem):
+    me = lax.axis_index("ka")
+    pb = lax.axis_index("pb")
+    size = lax.axis_size("ka")
+    barrier = pltpu.get_barrier_semaphore()
+    for d in range(1, size):
+        pl.semaphore_signal(barrier, inc=1, device_id=(pb, ka_peer(d)), device_id_type=MESH)
+    own = pltpu.make_async_copy(x_ref, o_ref.at[me], local_sem)
+    own.start()
+    pl.semaphore_wait(barrier, size - 1)
+    copies = []
+    for d in range(1, size):
+        copy = pltpu.make_async_remote_copy(
+            src_ref=x_ref,
+            dst_ref=o_ref.at[me],
+            send_sem=send_sem.at[d - 1],
+            recv_sem=recv_sem.at[d - 1],
+            device_id=(pb, ka_peer(d)),
+            device_id_type=MESH,
+        )
+        copy.start()
+        copies.append(copy)
+    own.wait()
+    for copy in copies:
+        copy.wait()
+
+
+def gather_call(x):
+    size = lax.axis_size("ka")
+    vmem = pl.BlockSpec(memory_space=pltpu.VMEM)
+    return pl.pallas_call(
+        gather_kernel,
+        out_shape=jax.ShapeDtypeStruct((size,) + x.shape, x.dtype),
+        in_specs=[vmem],
+        out_specs=vmem,
+        scratch_shapes=[
+            pltpu.SemaphoreType.DMA,
+            pltpu.SemaphoreType.DMA((size - 1,)),
+            pltpu.SemaphoreType.DMA((size - 1,)),
+        ],
+        compiler_params=pltpu.CompilerParams(
+            collective_id=0, has_side_effects=True, vmem_limit_bytes=16 << 20
+        ),
+    )(x)
+
+
 def pair_kernel(
     tok_ref, key_ref, trunk_ref, w_rel_ref, cat_gain_ref, w_in_ref, trans_gain_ref, ab_ref,
-    out_ref, bias_gain_ref, w_bias_ref, pair_ref, bias_ref, wrel_scr, bias_scr,
+    out_ref, bias_gain_ref, w_bias_ref, kv_ref, pair_ref, bias_out_ref, kv_out_ref, wrel_scr,
+    bias_scr, bias_ref, local_sem, ring_send, ring_recv, bias_send, bias_recv,
 ):
     q_rows, keys = trunk_ref.shape[0], trunk_ref.shape[1]
-    q_start = lax.axis_index("pb") * q_rows
-    k_start = lax.axis_index("ka") * keys
+    n = lax.axis_size("pb")
+    size = lax.axis_size("ka")
+    pb = lax.axis_index("pb")
+    ka = lax.axis_index("ka")
+    pos = ring_position(pb)
+    right, left = ring_index(pos + 1), ring_index(pos + n - 1)
+
+    barrier = pltpu.get_barrier_semaphore()
+    for side in (left, right):
+        pl.semaphore_signal(barrier, inc=1, device_id=(side, ka), device_id_type=MESH)
+    for d in range(1, size):
+        pl.semaphore_signal(barrier, inc=1, device_id=(pb, ka_peer(d)), device_id_type=MESH)
+    own = pltpu.make_async_copy(kv_ref, kv_out_ref.at[pb], local_sem.at[0])
+    own.start()
+    own.wait()
+
+    q_start = pb * q_rows
+    k_start = ka * keys
     wrel_scr[...] = jnp.zeros_like(wrel_scr)
     wrel_scr[0:REL, :] = w_rel_ref[...]
     k_pos = k_start + lax.broadcasted_iota(jnp.int32, key_ref.shape[1:], 0)
-
-    def step(i, carry):
+    pl.semaphore_wait(barrier, 2 + size - 1)
+
+    def to_right(s):
+        slot = kv_out_ref.at[ring_index(pos + n - s)]
+        return pltpu.make_async_remote_copy(
+            src_ref=slot, dst_ref=slot, send_sem=ring_send.at[0, s], recv_sem=ring_recv.at[0, s],
+            device_id=(right, ka), device_id_type=MESH,
+        )
+
+    def to_left(s):
+        slot = kv_out_ref.at[ring_index(pos + s)]
+        return pltpu.make_async_remote_copy(
+            src_ref=slot, dst_ref=slot, send_sem=ring_send.at[1, s], recv_sem=ring_recv.at[1, s],
+            device_id=(left, ka), device_id_type=MESH,
+        )
+
+    def pair_step(i):
         pair_block(
             pl.multiple_of(i * ROWS, ROWS), q_start, k_pos, tok_ref, key_ref, trunk_ref, wrel_scr,
             cat_gain_ref, w_in_ref, trans_gain_ref, ab_ref, out_ref, bias_gain_ref, w_bias_ref,
             pair_ref, bias_scr, bias_ref,
         )
+
+    blocks = q_rows // ROWS
+    rights, lefts = n // 2, n - 1 - n // 2
+    both = min(blocks, lefts)
+
+    def with_pair(s, carry):
+        a, b = to_right(s), to_left(s)
+        a.start()
+        b.start()
+        pair_step(s)
+        a.wait()
+        b.wait()
         return carry
 
-    lax.fori_loop(0, q_rows // ROWS, step, 0)
-
-
-def pair_call(token_ids, key_cols, trunk, w_rel, cat_gain, w_in, trans_gain, ab, out, bias_gain, w_bias):
+    lax.fori_loop(0, both, with_pair, 0)
+    for i in range(both, blocks):
+        pair_step(i)
+
+    heads_local = bias_out_ref.shape[1]
+    copies = [
+        pltpu.make_async_copy(
+            bias_ref.at[pl.ds(ka * heads_local, heads_local)], bias_out_ref.at[ka], local_sem.at[1]
+        )
+    ]
+    for d in range(1, size):
+        peer = ka_peer(d)
+        copies.append(
+            pltpu.make_async_remote_copy(
+                src_ref=bias_ref.at[pl.ds(peer * heads_local, heads_local)],
+                dst_ref=bias_out_ref.at[ka],
+                send_sem=bias_send.at[d - 1],
+                recv_sem=bias_recv.at[d - 1],
+                device_id=(pb, peer),
+                device_id_type=MESH,
+            )
+        )
+    for copy in copies:
+        copy.start()
+
+    def only_ring(s, carry):
+        a, b = to_right(s), to_left(s)
+        a.start()
+        b.start()
+        a.wait()
+        b.wait()
+        return carry
+
+    if lefts > both:
+        lax.fori_loop(both, lefts, only_ring, 0)
+    for s in range(lefts, rights):
+        last = to_right(s)
+        last.start()
+        last.wait()
+    for copy in copies:
+        copy.wait()
+
+
+def pair_call(token_ids, key_cols, trunk, w_rel, cat_gain, w_in, trans_gain, ab, out, bias_gain, w_bias, kv):
     q_rows, keys, c = trunk.shape
     heads = w_bias.shape[1]
+    n, size = lax.axis_size("pb"), lax.axis_size("ka")
     vmem = pl.BlockSpec(memory_space=pltpu.VMEM)
     return pl.pallas_call(
         pair_kernel,
         out_shape=(
             jax.ShapeDtypeStruct((q_rows, keys, c), BF16),
-            jax.ShapeDtypeStruct((heads, q_rows, keys), BF16),
+            jax.ShapeDtypeStruct((size, heads // size, q_rows, keys), BF16),
+            jax.ShapeDtypeStruct((n,) + kv.shape, BF16),
         ),
-        in_specs=[pl.BlockSpec(memory_space=pltpu.SMEM)] + [vmem] * 10,
-        out_specs=(vmem, vmem),
-        scratch_shapes=[pltpu.VMEM((256, c), BF16), pltpu.VMEM((heads, ROWS, keys), F32)],
-        compiler_params=pltpu.CompilerParams(vmem_limit_bytes=40 << 20),
+        in_specs=[pl.BlockSpec(memory_space=pltpu.SMEM)] + [vmem] * 11,
+        out_specs=(vmem, vmem, vmem),
+        scratch_shapes=[
+            pltpu.VMEM((256, c), BF16),
+            pltpu.VMEM((heads, ROWS, keys), F32),
+            pltpu.VMEM((heads, q_rows, keys), BF16),
+            pltpu.SemaphoreType.DMA((2,)),
+            pltpu.SemaphoreType.DMA((2, n // 2)),
+            pltpu.SemaphoreType.DMA((2, n // 2)),
+            pltpu.SemaphoreType.DMA((size - 1,)),
+            pltpu.SemaphoreType.DMA((size - 1,)),
+        ],
+        compiler_params=pltpu.CompilerParams(
+            collective_id=1, has_side_effects=True, vmem_limit_bytes=48 << 20
+        ),
         cost_estimate=pl.CostEstimate(flops=2300000000, bytes_accessed=4000000, transcendentals=0),
     )(token_ids, key_cols, trunk, w_rel, cat_gain.reshape(1, -1), w_in, trans_gain, ab, out,
-      bias_gain.reshape(1, -1), w_bias)
+      bias_gain.reshape(1, -1), w_bias, kv)
+
+
+def reduce_kernel(x_ref, w_ref, o_ref, part, got, send_sem, recv_sem):
+    me = lax.axis_index("ka")
+    pb = lax.axis_index("pb")
+    size = lax.axis_size("ka")
+    width = part.shape[2]
+    barrier = pltpu.get_barrier_semaphore()
+    for d in range(1, size):
+        pl.semaphore_signal(barrier, inc=1, device_id=(pb, ka_peer(d)), device_id_type=MESH)
+    whole = dot(x_ref[...], w_ref[...]).astype(BF16)
+    for j in range(size):
+        part[j] = whole[:, j * width : (j + 1) * width]
+    pl.semaphore_wait(barrier, size - 1)
+    copies = []
+    for d in range(1, size):
+        peer = ka_peer(d)
+        copy = pltpu.make_async_remote_copy(
+            src_ref=part.at[peer],
+            dst_ref=got.at[d - 1],
+            send_sem=send_sem.at[d - 1],
+            recv_sem=recv_sem.at[d - 1],
+            device_id=(pb, peer),
+            device_id_type=MESH,
+        )
+        copy.start()
+        copies.append(copy)
+    total = part[me].astype(F32)
+    for d, copy in enumerate(copies):
+        copy.wait()
+        total = total + got[d].astype(F32)
+    o_ref[...] = total.astype(BF16)
+
+
+def reduce_call(x, w):
+    size = lax.axis_size("ka")
+    rows, width = x.shape[0], w.shape[1] // size
+    vmem = pl.BlockSpec(memory_space=pltpu.VMEM)
+    return pl.pallas_call(
+        reduce_kernel,
+        out_shape=jax.ShapeDtypeStruct((rows, width), BF16),
+        in_specs=[vmem, vmem],
+        out_specs=vmem,
+        scratch_shapes=[
+            pltpu.VMEM((size, rows, width), BF16),
+            pltpu.VMEM((size - 1, rows, width), BF16),
+            pltpu.SemaphoreType.DMA((size - 1,)),
+            pltpu.SemaphoreType.DMA((size - 1,)),
+        ],
+        compiler_params=pltpu.CompilerParams(
+            collective_id=2, has_side_effects=True, vmem_limit_bytes=32 << 20
+        ),
+    )(x, w)
 
 
 def soft_weights(logits):
@@ -185,28 +405,28 @@
     k_start = lax.axis_index("ka") * k_rows
     key_ids = lax.dynamic_slice_in_dim(token_ids, k_start, k_rows, 1)
     key_cols = jnp.broadcast_to(key_ids[:, :, None], (3, k_rows, 128))
-    pair_cond, bias_tile = pair_call(
-        token_ids, key_cols, pair_trunk, w_rel, cat_gain, w_in, trans_gain, trans_ab, trans_out,
-        bias_gain, w_bias,
-    )
     samples = normed.shape[0]
     feat_local = normed.shape[2]
     heads_local = feat_local // HD
+    ka_size = lax.axis_size("ka")
     scale_factor = 1.0 / math.sqrt(HD)
-    projected = jnp.einsum(
-        "sqf,pfe->psqe",
-        lax.all_gather(normed, "ka", axis=2, tiled=True),
-        w_proj,
-        preferred_element_type=jnp.float32,
-    )
+    slots = gather_call(normed)
+    full = jnp.transpose(slots, (1, 2, 0, 3)).reshape(samples, q_rows, ka_size * feat_local)
+    projected = jnp.einsum("sqf,pfe->psqe", full, w_proj, preferred_element_type=jnp.float32)
+    kv = jnp.concatenate(
+        [projected[1].astype(BF16), projected[2].astype(BF16)], axis=-1
+    ).reshape(samples * q_rows, 2 * feat_local)
+    pair_cond, bias_slots, kv_all = pair_call(
+        token_ids, key_cols, pair_trunk, w_rel, cat_gain, w_in, trans_gain, trans_ab, trans_out,
+        bias_gain, w_bias, kv,
+    )
+    bias_rows = jnp.transpose(bias_slots, (1, 2, 0, 3)).reshape(heads_local, q_rows, -1)
     queries = projected[0].astype(jnp.bfloat16).reshape(samples, q_rows, heads_local, HD)
-    kv_local = jnp.transpose(
-        jnp.stack([projected[1], projected[2]], axis=1).astype(jnp.bfloat16), (0, 1, 3, 2)
-    )
-    bias_rows = lax.all_to_all(bias_tile, "ka", split_axis=0, concat_axis=2, tiled=True)
-    kv_all = lax.all_gather(kv_local, "pb", axis=3, tiled=True)
-    keys_all = kv_all[:, 0].reshape(samples, heads_local, HD, kv_all.shape[3])
-    values_all = kv_all[:, 1].reshape(samples, heads_local, HD, kv_all.shape[3])
+    tokens = kv_all.shape[0] * q_rows
+    kv_heads = kv_all.reshape(-1, samples, q_rows, 2, heads_local, HD)
+    kv_heads = jnp.transpose(kv_heads, (3, 1, 4, 5, 0, 2))
+    kv_heads = kv_heads.reshape(2, samples, heads_local, HD, tokens)
+    keys_all, values_all = kv_heads[0], kv_heads[1]
     logits = (
         jnp.einsum("sqhd,shdk->shqk", queries, keys_all, preferred_element_type=jnp.float32)
         * scale_factor
@@ -219,17 +439,8 @@
     gated_result = (
         attended.reshape(samples, q_rows, feat_local) * jax.nn.sigmoid(projected[3])
     ).astype(jnp.bfloat16)
-    flat_gated = gated_result.reshape(samples * q_rows, feat_local)
-    summed = lax.psum_scatter(
-        jnp.einsum(
-            "fe,nf->en", output_weight, flat_gated, preferred_element_type=jnp.float32
-        ).astype(jnp.bfloat16),
-        "ka",
-        scatter_dimension=0,
-        tiled=True,
-    ).astype(jnp.float32)
-    update = jnp.transpose(summed).reshape(samples, q_rows, feat_local).astype(jnp.bfloat16)
-    return (pair_cond, update)
+    update = reduce_call(gated_result.reshape(samples * q_rows, feat_local), output_weight)
+    return (pair_cond, update.reshape(samples, q_rows, feat_local))
 
 
 def solution(mesh):

time: 133 us -> 130 us (0.977)
  waiting for transfers between devices: 61.4 us -> 0 us
  local copies, waits for them, and re-layouts: 15.4 us -> 60.8 us
  Pallas kernels: 13.3 us -> 57.7 us
  blocking collectives: 14.2 us -> 0 us
  between operations: 14.2 us -> 0.82 us
  starting transfers between devices: 3.53 us -> 0 us
  matrix products: 8.23 us -> 6.29 us
    all_gather x1 -> x0, waiting for transfers between devices: 35.8 us -> none  [shards(): kv_all = lax.all_gather(kv_local, 'pb', axis=3, tiled=True)]
    pallas_call x0 -> x2, Pallas kernels: none -> 25.8 us  [the longest x1 13.6 us: reduce_call(): pl.pallas_call(reduce_kernel, out_shape=jax.ShapeDtypeStruct((rows, width...]
    unnamed x3 -> x0, waiting for transfers between devices: 22.5 us -> none
    pallas_call x1, Pallas kernels: 13.3 us -> 32 us  [pair_call(): pl.pallas_call(pair_kernel, out_shape=(jax.ShapeDtypeStruct((q_rows, keys...]
    slice x3, local copies, waits for them, and re-layouts: 7.35 us -> 22.4 us  [shards(): keys_all, values_all = (kv_heads[0], kv_heads[1])]
    all_gather x1 -> x0, blocking collectives: 14.2 us -> none  [shards(): lax.all_gather(normed, 'ka', axis=2, tiled=True)]
    squeeze x0 -> x2, local copies, waits for them, and re-layouts: none -> 8.94 us  [shards(): keys_all, values_all = (kv_heads[0], kv_heads[1])]
    unnamed x30 -> x41, local copies, waits for them, and re-layouts: 4.67 us -> 13.1 us
  transfers between devices with their start and end apart: 3 -> 0, of which waited for: 3 -> 0; matrix products, arithmetic and copies ran while one was open for 2% -> 0% of each run, Pallas kernels for 10% -> 0%
where the time goes in v2:
time: 130 us; the launch traced here: 129 us
  local copies, waits for them, and re-layouts  60.8 us (47%)
  Pallas kernels  57.7 us (44%)
  matrix products  6.29 us (5%)
  other arithmetic  2.9 us (2%)
    pallas_call x1, Pallas kernels, pair_call(): pl.pallas_call(pair_kernel, out_shape=(jax.ShapeDtypeStruct((q_rows, keys...  32 us
    slice x3, local copies, waits for them, and re-layouts, shards(): keys_all, values_all = (kv_heads[0], kv_heads[1])  22.4 us
    pallas_call x1, Pallas kernels, reduce_call(): pl.pallas_call(reduce_kernel, out_shape=jax.ShapeDtypeStruct((rows, width...  13.6 us
    unnamed x41, local copies, waits for them, and re-layouts  13.1 us
    pallas_call x1, Pallas kernels, gather_call(): pl.pallas_call(gather_kernel, out_shape=jax.ShapeDtypeStruct((size,) + x....  12.1 us
    squeeze x2, local copies, waits for them, and re-layouts, shards(): keys_all, values_all = (kv_heads[0], kv_heads[1])  8.94 us
    reshape x1, local copies, waits for them, and re-layouts, shards(): kv_heads = kv_all.reshape(-1, samples, q_rows, 2, heads_local, HD)  6.88 us
    dot_general x1, matrix products, shards(): jnp.einsum('shqk,shdk->sqhd', weights, values_all, preferred_element_type...  3.23 us

profile of v2, /device:TPU:1, one launch (start us, length us, event | category | flops | bytes accessed | tf_op | source)
XLA Modules:
  0.0 128.6 jit_solution(8978522828566487504)
XLA Ops:
  0.6 0.0 copy-start
  0.6 0.9 constant_dynamic-slice_fusion
  1.5 1.4 %copy.21.w_bias_ref = bf16[128,16]{1,0:T(8,128)(2,1)} copy(bf16[128,16]{0,1:T(8,128)(2,1)} %param.22) | data formatting | bytes 8192 | tf_op args[9]
  2.9 0.8 broadcast_in_dim.2.key_ref
  3.7 0.9 copy-done.5
  4.6 12.1 %shard_map.140 = bf16[4,8,48,192]{3,2,1,0:T(8,128)(2,1)S(1)} custom-call(bf16[8,48,192]{2,1,0:T(8,128)(2,1)S(1)} %copy-done.5), custom_call_target="tpu_custom_call" | custom-call | tf_op jit(solution)/shard_map/pallas_call | solution.py:175
  16.8 0.6 copy.20
  17.4 0.7 reshape.66
  18.1 0.0 copy-done
  18.1 0.8 fusion.20
  18.9 0.0 copy-start.8
  18.9 0.0 copy-start.14
  18.9 0.0 copy-start.15
  19.0 0.8 pad_maximum_fusion.kv_ref
  19.8 1.0 convert_element_type.38
  20.8 0.9 fusion.7
  21.7 0.0 copy-done.8
  21.7 0.0 copy-done.14
  21.7 0.0 copy-done.15
  21.7 1.0 copy-done.4
  22.7 0.9 copy-done.6
  23.6 0.8 copy-done.7
  24.3 1.3 copy-done.9
  25.6 0.9 copy-done.10
  26.5 0.9 copy-done.11
  27.5 0.8 copy-done.12
  28.3 0.8 copy-done.13
  29.1 0.7 copy-done.16
  29.7 32.0 %shard_map.141 = (bf16[48,96,128]{2,1,0:T(8,128)(2,1)S(1)}, bf16[4,4,48,96]{3,2,1,0:T(8,128)(2,1)S(1)}, bf16[8,384,384]{2,1,0:T(8,128)(2,1)S(1)}) custom-call(s32[3,384]{1,0:T(4,128)S(1)} %copy-done.8, s32[3,96,128]{2,1,0:T(8,128)S(1)} %copy-done.6, bf16[48,96,128]{2,1,0:T(8,128)(2,1)S(1)} %copy-done.9, bf16[139,128]{1,0:T(8,128)(2,1)S(1)} %copy-done.13, ...), custom_call_target="tpu_custom_call" | custom-call | flops 2300000000 | bytes 4000000 | tf_op jit(solution)/shard_map/pallas_call | solution.py:302
  61.7 0.0 copy-start.1
  61.7 1.0 copy-done.1
  62.7 1.0 copy.25
  63.7 1.9 %reshape.64 = f32[4,48,384]{2,1,0:T(8,128)} reshape(f32[4,48,4,96]{3,2,1,0:T(4,128)} %copy.25) | data formatting | bytes 589824 | tf_op jit(solution)/shard_map/convert_element_type | solution.py:434
  65.7 6.9 %reshape.61 = bf16[8,8,48,2,4,48]{5,4,3,2,1,0:T(4,128)(2,1)} reshape(bf16[8,384,384]{2,1,0:T(8,128)(2,1)S(1)} %get-tuple-element.6) | data formatting | bytes 4718592 | tf_op jit(solution)/shard_map/reshape | solution.py:426
  72.5 8.0 %fusion.18 = (bf16[1,8,4,48,8,48]{3,2,0,5,1,4:T(4,128)(2,1)}, bf16[1,8,4,48,8,48]{3,2,0,5,1,4:T(4,128)(2,1)}) fusion(bf16[2,8,4,48,8,48]{3,2,0,5,1,4:T(4,128)(2,1)} %bitcast.37), kind=kLoop, calls=%fused_computation.22 | loop fusion | bytes 4718592 | tf_op jit(solution)/shard_map/slice | solution.py:429
  80.5 7.2 %copy.23 = bf16[1,8,4,48,8,48]{5,4,3,2,1,0:T(8,128)(2,1)} copy(bf16[1,8,4,48,8,48]{3,2,0,5,1,4:T(4,128)(2,1)} %get-tuple-element.8) | data formatting | bytes 2359296 | tf_op jit(solution)/shard_map/slice | solution.py:429
  87.7 4.5 %squeeze.5 = bf16[8,4,48,384]{3,2,1,0:T(8,128)(2,1)S(1)} reshape(bf16[1,8,4,48,8,48]{5,4,3,2,1,0:T(8,128)(2,1)} %copy.23) | data formatting | bytes 2359296 | tf_op jit(solution)/shard_map/squeeze | solution.py:429
  92.3 2.3 %fusion.21 = (f32[8,4,48]{2,1,0:T(4,128)S(1)}, f32[8,4,48,384]{3,2,1,0:T(8,128)}) fusion(f32[4,48,384]{2,1,0:T(8,128)S(1)} %copy-done.18, bf16[8,4,48,384]{3,2,1,0:T(8,128)(2,1)S(1)} %squeeze.5, bf16[8,48,4,48]{3,2,1,0:T(4,128)(2,1)S(1)} %copy-done.17), kind=kOutput, calls=%fused_computation.25 | convolution fusion | flops 58982784 | bytes 3987456 | tf_op jit(solution)/shard_map/sub | solution.py:384
  94.5 7.2 %copy.22 = bf16[1,8,4,48,8,48]{5,4,3,2,1,0:T(8,128)(2,1)} copy(bf16[1,8,4,48,8,48]{3,2,0,5,1,4:T(4,128)(2,1)} %get-tuple-element.9) | data formatting | bytes 2359296 | tf_op jit(solution)/shard_map/slice | solution.py:429
  101.7 4.4 %squeeze.4 = bf16[8,4,48,384]{3,2,1,0:T(8,128)(2,1)S(1)} reshape(bf16[1,8,4,48,8,48]{5,4,3,2,1,0:T(8,128)(2,1)} %copy.22) | data formatting | bytes 2359296 | tf_op jit(solution)/shard_map/squeeze | solution.py:429
  106.2 3.2 %convolution_bitcast_fusion.1 = f32[8,48,4,48]{1,3,2,0:T(8,128)} fusion(bf16[8,4,48,384]{3,2,1,0:T(8,128)(2,1)S(1)} %squeeze.4, f32[8,4,48,384]{3,2,1,0:T(8,128)} %get-tuple-element.16, f32[8,4,48]{2,1,0:T(4,128)S(1)} %get-tuple-element.15), kind=kOutput, calls=%fused_computation.6 | convolution fusion | flops 57802752 | bytes 3840000 | tf_op jit(solution)/shard_map/shqk,shdk->sqhd/dot_general | solution.py:436
  109.4 1.6 %copy.29 = f32[8,48,4,48]{3,2,1,0:T(4,128)S(1)} copy(f32[8,48,4,48]{1,3,2,0:T(8,128)} %convolution_bitcast_fusion.1) | data formatting | bytes 589824 | tf_op jit(solution)/shard_map/reshape | solution.py:440
  110.9 1.1 reshape.68
  112.1 1.2 fusion.8.x_ref
  113.2 13.6 %shard_map.142 = bf16[384,192]{1,0:T(8,128)(2,1)S(1)} custom-call(bf16[384,192]{1,0:T(8,128)(2,1)S(1)} %fusion.8.x_ref, bf16[192,768]{1,0:T(8,128)(2,1)S(1)} %copy-done.3), custom_call_target="tpu_custom_call" | custom-call | tf_op jit(solution)/shard_map/pallas_call | solution.py:365
  126.9 0.0 copy-done.2
  126.9 1.0 copy.43
  127.9 0.7 copy.44
  (19 shorter events, 0.1 us)
Async XLA Ops:
  0.6 17.4 %copy-start = (bf16[4,768,192]{1,2,0:T(8,128)(2,1)S(1)}, bf16[4,768,192]{1,2,0:T(8,128)(2,1)}, u32[]{:S(2)}) copy-start(bf16[4,768,192]{1,2,0:T(8,128)(2,1)} %param.24) | copy-start | bytes 3538948
  3.7 0.9 copy-start.5
  18.9 2.8 %copy-start.8 = (s32[3,384]{1,0:T(4,128)S(1)}, s32[3,384]{1,0:T(4,128)}, u32[]{:S(2)}) copy-start(s32[3,384]{1,0:T(4,128)} %tok_ref.1) | copy-start | bytes 13828
  18.9 2.8 %copy-start.14 = (f32[256]{0:T(256)S(1)}, f32[256]{0:T(256)}, u32[]{:S(2)}) copy-start(f32[256]{0:T(256)} %param.16) | copy-start | bytes 3076
  18.9 2.8 %copy-start.15 = (f32[2,128]{1,0:T(2,128)S(1)}, f32[2,128]{1,0:T(2,128)}, u32[]{:S(2)}) copy-start(f32[2,128]{1,0:T(2,128)} %trans_gain_ref.1) | copy-start | bytes 3076
  21.7 1.0 copy-start.4
  22.7 0.9 copy-start.6
  23.6 0.8 copy-start.7
  24.3 1.3 copy-start.9
  25.6 0.9 copy-start.10
  26.5 0.9 copy-start.11
  27.4 0.8 copy-start.12
  28.3 0.8 copy-start.13
  29.1 0.7 copy-start.16
  61.7 1.0 copy-start.1
  87.7 4.5 %copy-start.17 = (bf16[8,48,4,48]{3,2,1,0:T(4,128)(2,1)S(1)}, bf16[8,48,4,48]{3,2,1,0:T(4,128)(2,1)}, u32[]{:S(2)}) copy-start(bf16[8,48,4,48]{3,2,1,0:T(4,128)(2,1)} %convert_element_type.38) | copy-start | bytes 442372
  87.7 4.5 %copy-start.18 = (f32[4,48,384]{2,1,0:T(8,128)S(1)}, f32[4,48,384]{2,1,0:T(8,128)}, u32[]{:S(2)}) copy-start(f32[4,48,384]{2,1,0:T(8,128)} %reshape.64) | copy-start | bytes 884740
  109.4 3.8 %copy-start.3 = (bf16[192,768]{1,0:T(8,128)(2,1)S(1)}, bf16[192,768]{1,0:T(8,128)(2,1)}, u32[]{:S(2)}) copy-start(bf16[192,768]{1,0:T(8,128)(2,1)} %w_ref.1) | copy-start | bytes 884740
  109.4 17.5 %copy-start.2 = (bf16[48,96,128]{2,1,0:T(8,128)(2,1)S(1)}, bf16[48,96,128]{2,1,0:T(8,128)(2,1)}, u32[]{:S(2)}) copy-start(bf16[48,96,128]{2,1,0:T(8,128)(2,1)} %copy-done.1) | copy-start | bytes 3538948

commit v3 on v2

--- a/solution.py
+++ b/solution.py
@@ -142,21 +142,24 @@
     return jnp.where(lax.rem(index, 2) == 0, half, n - 1 - half)
 
 
-def gather_kernel(x_ref, o_ref, local_sem, send_sem, recv_sem):
+def pad128(v):
+    return -(-v // 128) * 128
+
+
+def gather_kernel(x_ref, w_ref, q_ref, kv_ref, gate_ref, got, send_sem, recv_sem):
     me = lax.axis_index("ka")
     pb = lax.axis_index("pb")
     size = lax.axis_size("ka")
+    samples, q_rows, feat = x_ref.shape
     barrier = pltpu.get_barrier_semaphore()
     for d in range(1, size):
         pl.semaphore_signal(barrier, inc=1, device_id=(pb, ka_peer(d)), device_id_type=MESH)
-    own = pltpu.make_async_copy(x_ref, o_ref.at[me], local_sem)
-    own.start()
     pl.semaphore_wait(barrier, size - 1)
     copies = []
     for d in range(1, size):
         copy = pltpu.make_async_remote_copy(
             src_ref=x_ref,
-            dst_ref=o_ref.at[me],
+            dst_ref=got.at[d - 1],
             send_sem=send_sem.at[d - 1],
             recv_sem=recv_sem.at[d - 1],
             device_id=(pb, ka_peer(d)),
@@ -164,35 +167,64 @@
         )
         copy.start()
         copies.append(copy)
-    own.wait()
-    for copy in copies:
-        copy.wait()
-
-
-def gather_call(x):
+
+    def part(x, owner):
+        rows = pl.ds(pl.multiple_of(owner * feat, 16), feat)
+        x = x.reshape(samples * q_rows, feat)
+        return [dot(x, w_ref[p, rows, :]) for p in range(4)]
+
+    sums = part(x_ref[...], me)
+    for d in range(1, size):
+        copies[d - 1].wait()
+        more = part(got[d - 1], ka_peer(size - d))
+        sums = [u + v for u, v in zip(sums, more)]
+    q_ref[...] = jnp.zeros_like(q_ref)
+    q_ref[:, :feat] = sums[0].astype(BF16)
+    kv_ref[:, :feat] = sums[1].astype(BF16)
+    kv_ref[:, feat:] = sums[2].astype(BF16)
+    gate_ref[...] = sums[3]
+
+
+def gather_call(x, w_proj):
     size = lax.axis_size("ka")
+    samples, q_rows, feat = x.shape
+    rows = samples * q_rows
     vmem = pl.BlockSpec(memory_space=pltpu.VMEM)
     return pl.pallas_call(
         gather_kernel,
-        out_shape=jax.ShapeDtypeStruct((size,) + x.shape, x.dtype),
-        in_specs=[vmem],
-        out_specs=vmem,
+        out_shape=(
+            jax.ShapeDtypeStruct((rows, min(2 * feat, pad128(feat))), BF16),
+            jax.ShapeDtypeStruct((rows, 2 * feat), BF16),
+            jax.ShapeDtypeStruct((rows, feat), F32),
+        ),
+        in_specs=[vmem, vmem],
+        out_specs=(vmem, vmem, vmem),
         scratch_shapes=[
-            pltpu.SemaphoreType.DMA,
+            pltpu.VMEM((size - 1,) + x.shape, BF16),
             pltpu.SemaphoreType.DMA((size - 1,)),
             pltpu.SemaphoreType.DMA((size - 1,)),
         ],
         compiler_params=pltpu.CompilerParams(
-            collective_id=0, has_side_effects=True, vmem_limit_bytes=16 << 20
+            collective_id=0, has_side_effects=True, vmem_limit_bytes=24 << 20
         ),
-    )(x)
+    )(x, w_proj)
 
 
 def pair_kernel(
-    tok_ref, key_ref, trunk_ref, w_rel_ref, cat_gain_ref, w_in_ref, trans_gain_ref, ab_ref,
-    out_ref, bias_gain_ref, w_bias_ref, kv_ref, pair_ref, bias_out_ref, kv_out_ref, wrel_scr,
-    bias_scr, bias_ref, local_sem, ring_send, ring_recv, bias_send, bias_recv,
+    tok_ref, *refs
 ):
+    sources, refs = refs[:10], refs[10:]
+    kv_ref, pair_ref, bias_out_ref, kv_out_ref = refs[:4]
+    wrel_scr, bias_scr, bias_ref, local_sem, ring_send, ring_recv, bias_send, bias_recv = refs[4:12]
+    fetch_sem, held = refs[12], refs[13:]
+    fetches = [
+        pltpu.make_async_copy(src, dst, fetch_sem.at[i])
+        for i, (src, dst) in enumerate(zip(sources, held))
+    ]
+    for fetch in fetches:
+        fetch.start()
+    (key_ref, trunk_ref, w_rel_ref, cat_gain_ref, w_in_ref, trans_gain_ref, ab_ref, out_ref,
+     bias_gain_ref, w_bias_ref) = held
     q_rows, keys = trunk_ref.shape[0], trunk_ref.shape[1]
     n = lax.axis_size("pb")
     size = lax.axis_size("ka")
@@ -209,6 +241,8 @@
     own = pltpu.make_async_copy(kv_ref, kv_out_ref.at[pb], local_sem.at[0])
     own.start()
     own.wait()
+    for fetch in fetches:
+        fetch.wait()
 
     q_start = pb * q_rows
     k_start = ka * keys
@@ -299,6 +333,9 @@
     heads = w_bias.shape[1]
     n, size = lax.axis_size("pb"), lax.axis_size("ka")
     vmem = pl.BlockSpec(memory_space=pltpu.VMEM)
+    fetched = (key_cols, trunk, w_rel, cat_gain.reshape(1, -1), w_in, trans_gain, ab, out,
+               bias_gain.reshape(1, -1), w_bias)
+    hbm = pl.BlockSpec(memory_space=pltpu.HBM)
     return pl.pallas_call(
         pair_kernel,
         out_shape=(
@@ -306,7 +343,7 @@
             jax.ShapeDtypeStruct((size, heads // size, q_rows, keys), BF16),
             jax.ShapeDtypeStruct((n,) + kv.shape, BF16),
         ),
-        in_specs=[pl.BlockSpec(memory_space=pltpu.SMEM)] + [vmem] * 11,
+        in_specs=[pl.BlockSpec(memory_space=pltpu.SMEM)] + [hbm] * 10 + [vmem],
         out_specs=(vmem, vmem, vmem),
         scratch_shapes=[
             pltpu.VMEM((256, c), BF16),
@@ -317,16 +354,54 @@
             pltpu.SemaphoreType.DMA((2, n // 2)),
             pltpu.SemaphoreType.DMA((size - 1,)),
             pltpu.SemaphoreType.DMA((size - 1,)),
-        ],
+            pltpu.SemaphoreType.DMA((10,)),
+        ] + [pltpu.VMEM(v.shape, v.dtype) for v in fetched],
         compiler_params=pltpu.CompilerParams(
             collective_id=1, has_side_effects=True, vmem_limit_bytes=48 << 20
         ),
         cost_estimate=pl.CostEstimate(flops=2300000000, bytes_accessed=4000000, transcendentals=0),
-    )(token_ids, key_cols, trunk, w_rel, cat_gain.reshape(1, -1), w_in, trans_gain, ab, out,
-      bias_gain.reshape(1, -1), w_bias, kv)
-
-
-def reduce_kernel(x_ref, w_ref, o_ref, part, got, send_sem, recv_sem):
+    )(token_ids, *fetched, kv)
+
+
+def attend_sample(s, q_rows, q_ref, kv_ref, gate_ref, bias_scr, gated):
+    feat = gate_ref.shape[1]
+    heads = feat // HD
+    wide = q_ref.shape[1]
+    low = feat // 128 * 128
+    off = feat - low
+    tokens = kv_ref.shape[0] * q_rows
+    rows = pl.ds(pl.multiple_of(s * q_rows, 16), q_rows)
+    q = q_ref[rows, :].astype(F32)
+    lane = lax.broadcasted_iota(jnp.int32, q.shape, 1)
+    q_heads = jnp.concatenate(
+        [
+            jnp.where((lane >= h * HD) & (lane < (h + 1) * HD), q, 0.0).astype(BF16)
+            for h in range(heads)
+        ],
+        axis=0,
+    )
+    keys = kv_ref[:, rows, :wide].reshape(tokens, wide)
+    values = kv_ref[:, rows, low:].reshape(tokens, 2 * feat - low)
+    logits = lax.dot_general(
+        q_heads, keys, (((1,), (1,)), ((), ())), preferred_element_type=F32
+    )
+    logits = logits * (1.0 / math.sqrt(HD)) + bias_scr[...]
+    top = jnp.max(logits, axis=-1, keepdims=True)
+    powers = jnp.exp(logits - top)
+    inv = 1.0 / jnp.sum(powers, axis=-1, keepdims=True)
+    mixed = dot((powers * inv).astype(BF16), values)
+    lane = lax.broadcasted_iota(jnp.int32, (q_rows, 2 * feat - low), 1) - off
+    attended = jnp.zeros((q_rows, 2 * feat - low), F32)
+    for h in range(heads):
+        mine = mixed[h * q_rows : (h + 1) * q_rows]
+        attended = jnp.where((lane >= h * HD) & (lane < (h + 1) * HD), mine, attended)
+    gate = 0.5 + 0.5 * jnp.tanh(0.5 * gate_ref[rows, :])
+    gated[rows, :] = (attended[:, off:] * gate).astype(BF16)
+
+
+def reduce_kernel(
+    q_ref, kv_ref, gate_ref, bias_ref, w_ref, o_ref, bias_scr, gated, part, got, send_sem, recv_sem
+):
     me = lax.axis_index("ka")
     pb = lax.axis_index("pb")
     size = lax.axis_size("ka")
@@ -334,7 +409,20 @@
     barrier = pltpu.get_barrier_semaphore()
     for d in range(1, size):
         pl.semaphore_signal(barrier, inc=1, device_id=(pb, ka_peer(d)), device_id_type=MESH)
-    whole = dot(x_ref[...], w_ref[...]).astype(BF16)
+    keys = bias_ref.shape[3]
+    q_rows = bias_ref.shape[2]
+    for j in range(size):
+        bias_scr[:, j * keys : (j + 1) * keys] = (
+            bias_ref[j].reshape(bias_scr.shape[0], keys).astype(F32)
+        )
+
+    def step(i, carry):
+        for u in range(2):
+            attend_sample(2 * i + u, q_rows, q_ref, kv_ref, gate_ref, bias_scr, gated)
+        return carry
+
+    lax.fori_loop(0, gated.shape[0] // (2 * q_rows), step, 0)
+    whole = dot(gated[...], w_ref[...]).astype(BF16)
     for j in range(size):
         part[j] = whole[:, j * width : (j + 1) * width]
     pl.semaphore_wait(barrier, size - 1)
@@ -358,16 +446,19 @@
     o_ref[...] = total.astype(BF16)
 
 
-def reduce_call(x, w):
+def reduce_call(q, kv_all, gate, bias_slots, w):
     size = lax.axis_size("ka")
-    rows, width = x.shape[0], w.shape[1] // size
+    rows, width = gate.shape[0], w.shape[1] // size
+    heads, q_rows, keys = bias_slots.shape[1:]
     vmem = pl.BlockSpec(memory_space=pltpu.VMEM)
     return pl.pallas_call(
         reduce_kernel,
         out_shape=jax.ShapeDtypeStruct((rows, width), BF16),
-        in_specs=[vmem, vmem],
+        in_specs=[vmem] * 5,
         out_specs=vmem,
         scratch_shapes=[
+            pltpu.VMEM((heads * q_rows, size * keys), F32),
+            pltpu.VMEM(gate.shape, BF16),
             pltpu.VMEM((size, rows, width), BF16),
             pltpu.VMEM((size - 1, rows, width), BF16),
             pltpu.SemaphoreType.DMA((size - 1,)),
@@ -376,13 +467,7 @@
         compiler_params=pltpu.CompilerParams(
             collective_id=2, has_side_effects=True, vmem_limit_bytes=32 << 20
         ),
-    )(x, w)
-
-
-def soft_weights(logits):
-    row_max = jnp.max(logits, axis=-1, keepdims=True)
-    expweights = jnp.exp(logits - row_max)
-    return (expweights / jnp.sum(expweights, axis=-1, keepdims=True)).astype(jnp.bfloat16)
+    )(q, kv_all, gate, bias_slots, w)
 
 
 def shards(
@@ -407,39 +492,12 @@
     key_cols = jnp.broadcast_to(key_ids[:, :, None], (3, k_rows, 128))
     samples = normed.shape[0]
     feat_local = normed.shape[2]
-    heads_local = feat_local // HD
-    ka_size = lax.axis_size("ka")
-    scale_factor = 1.0 / math.sqrt(HD)
-    slots = gather_call(normed)
-    full = jnp.transpose(slots, (1, 2, 0, 3)).reshape(samples, q_rows, ka_size * feat_local)
-    projected = jnp.einsum("sqf,pfe->psqe", full, w_proj, preferred_element_type=jnp.float32)
-    kv = jnp.concatenate(
-        [projected[1].astype(BF16), projected[2].astype(BF16)], axis=-1
-    ).reshape(samples * q_rows, 2 * feat_local)
+    q, kv, gate = gather_call(normed, w_proj)
     pair_cond, bias_slots, kv_all = pair_call(
         token_ids, key_cols, pair_trunk, w_rel, cat_gain, w_in, trans_gain, trans_ab, trans_out,
         bias_gain, w_bias, kv,
     )
-    bias_rows = jnp.transpose(bias_slots, (1, 2, 0, 3)).reshape(heads_local, q_rows, -1)
-    queries = projected[0].astype(jnp.bfloat16).reshape(samples, q_rows, heads_local, HD)
-    tokens = kv_all.shape[0] * q_rows
-    kv_heads = kv_all.reshape(-1, samples, q_rows, 2, heads_local, HD)
-    kv_heads = jnp.transpose(kv_heads, (3, 1, 4, 5, 0, 2))
-    kv_heads = kv_heads.reshape(2, samples, heads_local, HD, tokens)
-    keys_all, values_all = kv_heads[0], kv_heads[1]
-    logits = (
-        jnp.einsum("sqhd,shdk->shqk", queries, keys_all, preferred_element_type=jnp.float32)
-        * scale_factor
-    )
-    logits = logits + bias_rows[None].astype(jnp.float32)
-    weights = soft_weights(logits)
-    attended = jnp.einsum(
-        "shqk,shdk->sqhd", weights, values_all, preferred_element_type=jnp.float32
-    )
-    gated_result = (
-        attended.reshape(samples, q_rows, feat_local) * jax.nn.sigmoid(projected[3])
-    ).astype(jnp.bfloat16)
-    update = reduce_call(gated_result.reshape(samples * q_rows, feat_local), output_weight)
+    update = reduce_call(q, kv_all, gate, bias_slots, output_weight)
     return (pair_cond, update.reshape(samples, q_rows, feat_local))
 
 

time: 130 us -> 66.9 us (0.51)
  local copies, waits for them, and re-layouts: 60.8 us -> 5.1 us
  matrix products: 6.29 us -> 0 us
  Pallas kernels: 57.7 us -> 60.8 us
  other arithmetic: 2.9 us -> 0 us
    slice x4 -> x0, local copies, waits for them, and re-layouts: 22.4 us -> none  [the longest x3 22.4 us: shards(): keys_all, values_all = (kv_heads[0], kv_heads[1])]
    reshape x4 -> x0, local copies, waits for them, and re-layouts: 10.2 us -> none  [the longest x1 6.88 us: shards(): kv_heads = kv_all.reshape(-1, samples, q_rows, 2, heads_local, HD)]
    squeeze x2 -> x0, local copies, waits for them, and re-layouts: 8.94 us -> none  [shards(): keys_all, values_all = (kv_heads[0], kv_heads[1])]
    unnamed x41 -> x26, local copies, waits for them, and re-layouts: 13.1 us -> 4.24 us
    dot_general x2 -> x0, matrix products: 4.02 us -> none  [the longest x1 3.23 us: shards(): jnp.einsum('shqk,shdk->sqhd', weights, values_all, preferred_element_type...]
    convert_element_type x3 -> x0, local copies, waits for them, and re-layouts: 3.92 us -> none  [the longest x2 2.92 us: shards(): logits = logits + bias_rows[None].astype(jnp.float32)]
    sub x1 -> x0, matrix products: 2.27 us -> none  [soft_weights(): expweights = jnp.exp(logits - row_max)]
    pallas_call x1, Pallas kernels: 13.6 us -> 15.3 us  [reduce_call(): pl.pallas_call(reduce_kernel, out_shape=jax.ShapeDtypeStruct((rows, width...]
where the time goes in v3:
time: 66.9 us; the launch traced here: 66.7 us
  Pallas kernels  60.8 us (91%)
  local copies, waits for them, and re-layouts  5.1 us (8%)
  between operations  0.85 us (1%)
    pallas_call x1, Pallas kernels, pair_call(): pl.pallas_call(pair_kernel, out_shape=(jax.ShapeDtypeStruct((q_rows, keys...  32.8 us
    pallas_call x1, Pallas kernels, reduce_call(): pl.pallas_call(reduce_kernel, out_shape=jax.ShapeDtypeStruct((rows, width...  15.3 us
    pallas_call x1, Pallas kernels, gather_call(): pl.pallas_call(gather_kernel, out_shape=(jax.ShapeDtypeStruct((rows, min(...  12.6 us
    unnamed x26, local copies, waits for them, and re-layouts  4.24 us

profile of v3, /device:TPU:1, one launch (start us, length us, event | category | flops | bytes accessed | tf_op | source)
XLA Modules:
  0.0 66.7 jit_solution(293095614150098800)
XLA Ops:
  0.6 0.8 %constant_dynamic-slice_fusion = s32[3,96]{1,0:T(4,128)S(1)} fusion(s32[3,384]{1,0:T(4,128)} %tok_ref.1, s32[]{:T(128)S(6)} %select_n.3), kind=kLoop, calls=%fused_computation | loop fusion | bytes 2308 | tf_op jit(solution)/shard_map/dynamic_slice | solution.py:491
  1.4 0.8 %copy.16.refs_9_ = bf16[128,16]{1,0:T(8,128)(2,1)S(1)} copy(bf16[128,16]{0,1:T(8,128)(2,1)} %param.22) | data formatting | bytes 8192 | tf_op args[9]
  2.2 0.1 broadcast_in_dim.2.refs_0_
  2.3 0.0 copy-start.1
  2.3 1.7 %copy.15.w_ref = bf16[4,768,192]{2,1,0:T(8,128)(2,1)S(1)} copy(bf16[4,768,192]{1,2,0:T(8,128)(2,1)} %param.24) | data formatting | bytes 2359296 | tf_op args[11]
  4.0 0.0 copy-done.1
  4.0 0.0 copy-start.2
  4.0 0.0 copy-start.3
  4.0 0.0 copy-start.4
  4.0 0.0 copy-start.5
  4.1 0.0 copy-start.6
  4.1 0.0 copy-start.7
  4.1 0.0 copy-start.8
  4.1 0.0 copy-start.9
  4.1 0.0 copy-start.10
  4.1 12.6 %shard_map.140 = (bf16[384,256]{1,0:T(8,128)(2,1)S(1)}, bf16[384,384]{1,0:T(8,128)(2,1)S(1)}, f32[384,192]{1,0:T(8,128)S(1)}) custom-call(bf16[8,48,192]{2,1,0:T(8,128)(2,1)S(1)} %copy-done.1, bf16[4,768,192]{2,1,0:T(8,128)(2,1)S(1)} %copy.15.w_ref), custom_call_target="tpu_custom_call" | custom-call | tf_op jit(solution)/shard_map/pallas_call | solution.py:193
  16.7 0.0 copy-done.2
  16.8 0.0 copy-done.3
  16.8 0.0 copy-done.4
  16.8 0.0 copy-done.5
  16.8 0.0 copy-done.6
  16.8 0.0 copy-done.7
  16.8 0.0 copy-done.8
  16.8 0.0 copy-done.9
  16.8 0.0 copy-done.10
  16.8 0.0 copy-start
  16.9 32.8 %shard_map.141 = (bf16[48,96,128]{2,1,0:T(8,128)(2,1)S(1)}, bf16[4,4,48,96]{3,2,1,0:T(8,128)(2,1)S(1)}, bf16[8,384,384]{2,1,0:T(8,128)(2,1)S(1)}) custom-call(s32[3,384]{1,0:T(4,128)S(1)} %copy-done.2, s32[3,96,128]{2,1,0:T(8,128)S(1)} %broadcast_in_dim.2.refs_0_, bf16[48,96,128]{2,1,0:T(8,128)(2,1)S(1)} %copy-done.3, bf16[139,128]{1,0:T(8,128)(2,1)S(1)} %copy-done.7, ...), custom_call_target="tpu_custom_call" | custom-call | flops 2300000000 | bytes 4000000 | tf_op jit(solution)/shard_map/pallas_call | solution.py:339
  49.7 0.0 copy-done
  49.7 15.3 %shard_map.142 = bf16[384,192]{1,0:T(8,128)(2,1)S(1)} custom-call(bf16[384,256]{1,0:T(8,128)(2,1)S(1)} %get-tuple-element.10.q_ref, bf16[8,384,384]{2,1,0:T(8,128)(2,1)S(1)} %get-tuple-element.11.kv_ref, f32[384,192]{1,0:T(8,128)S(1)} %get-tuple-element.12.gate_ref, bf16[4,4,48,96]{3,2,1,0:T(8,128)(2,1)S(1)} %get-tuple-element.13.bias_ref, ...), custom_call_target="tpu_custom_call" | custom-call | tf_op jit(solution)/shard_map/pallas_call | solution.py:454
  65.0 1.0 %copy.19 = bf16[48,96,128]{2,1,0:T(8,128)(2,1)} copy(bf16[48,96,128]{2,1,0:T(8,128)(2,1)S(1)} %get-tuple-element.16) | data formatting | bytes 2359296
  66.0 0.7 %copy.20 = bf16[8,48,192]{2,1,0:T(8,128)(2,1)} copy(bf16[8,48,192]{2,1,0:T(8,128)(2,1)S(1)} %bitcast.3) | data formatting | bytes 294912
Async XLA Ops:
  2.3 1.7 %copy-start.1 = (bf16[8,48,192]{2,1,0:T(8,128)(2,1)S(1)}, bf16[8,48,192]{2,1,0:T(8,128)(2,1)}, u32[]{:S(2)}) copy-start(bf16[8,48,192]{2,1,0:T(8,128)(2,1)} %x_ref.1) | copy-start | bytes 442372
  4.0 12.7 %copy-start.2 = (s32[3,384]{1,0:T(4,128)S(1)}, s32[3,384]{1,0:T(4,128)}, u32[]{:S(2)}) copy-start(s32[3,384]{1,0:T(4,128)} %tok_ref.1) | copy-start | bytes 13828
  4.0 12.7 %copy-start.3 = (bf16[48,96,128]{2,1,0:T(8,128)(2,1)S(1)}, bf16[48,96,128]{2,1,0:T(8,128)(2,1)}, u32[]{:S(2)}) copy-start(bf16[48,96,128]{2,1,0:T(8,128)(2,1)} %refs_1_.1) | copy-start | bytes 3538948
  4.0 12.7 %copy-start.4 = (bf16[2,128,512]{2,1,0:T(8,128)(2,1)S(1)}, bf16[2,128,512]{2,1,0:T(8,128)(2,1)}, u32[]{:S(2)}) copy-start(bf16[2,128,512]{2,1,0:T(8,128)(2,1)} %refs_6_.1) | copy-start | bytes 786436
  4.0 12.7 %copy-start.5 = (bf16[2,256,128]{2,1,0:T(8,128)(2,1)S(1)}, bf16[2,256,128]{2,1,0:T(8,128)(2,1)}, u32[]{:S(2)}) copy-start(bf16[2,256,128]{2,1,0:T(8,128)(2,1)} %refs_7_.1) | copy-start | bytes 393220
  4.1 12.7 %copy-start.6 = (bf16[256,128]{1,0:T(8,128)(2,1)S(1)}, bf16[256,128]{1,0:T(8,128)(2,1)}, u32[]{:S(2)}) copy-start(bf16[256,128]{1,0:T(8,128)(2,1)} %refs_4_.1) | copy-start | bytes 196612
  4.1 12.7 %copy-start.7 = (bf16[139,128]{1,0:T(8,128)(2,1)S(1)}, bf16[139,128]{1,0:T(8,128)(2,1)}, u32[]{:S(2)}) copy-start(bf16[139,128]{1,0:T(8,128)(2,1)} %refs_2_.1) | copy-start | bytes 106756
  4.1 12.7 %copy-start.8 = (f32[256]{0:T(256)S(1)}, f32[256]{0:T(256)}, u32[]{:S(2)}) copy-start(f32[256]{0:T(256)} %param.16) | copy-start | bytes 3076
  4.1 12.7 %copy-start.9 = (f32[2,128]{1,0:T(2,128)S(1)}, f32[2,128]{1,0:T(2,128)}, u32[]{:S(2)}) copy-start(f32[2,128]{1,0:T(2,128)} %refs_5_.1) | copy-start | bytes 3076
  4.1 12.7 %copy-start.10 = (f32[128]{0:T(128)S(1)}, f32[128]{0:T(128)}, u32[]{:S(2)}) copy-start(f32[128]{0:T(128)} %param.21) | copy-start | bytes 1540
  16.8 32.8 %copy-start = (bf16[192,768]{1,0:T(8,128)(2,1)S(1)}, bf16[192,768]{1,0:T(8,128)(2,1)}, u32[]{:S(2)}) copy-start(bf16[192,768]{1,0:T(8,128)(2,1)} %w_ref.2) | copy-start | bytes 884740

commit v4 on v3

--- a/solution.py
+++ b/solution.py
@@ -251,18 +251,18 @@
     k_pos = k_start + lax.broadcasted_iota(jnp.int32, key_ref.shape[1:], 0)
     pl.semaphore_wait(barrier, 2 + size - 1)
 
-    def to_right(s):
-        slot = kv_out_ref.at[ring_index(pos + n - s)]
+    half = kv_ref.shape[0] // 2
+
+    def hop(way, s, c):
+        owner = ring_index(pos + n - s) if way == 0 else ring_index(pos + s)
+        piece = kv_out_ref.at[owner, pl.ds(c * half, half)]
         return pltpu.make_async_remote_copy(
-            src_ref=slot, dst_ref=slot, send_sem=ring_send.at[0, s], recv_sem=ring_recv.at[0, s],
-            device_id=(right, ka), device_id_type=MESH,
-        )
-
-    def to_left(s):
-        slot = kv_out_ref.at[ring_index(pos + s)]
-        return pltpu.make_async_remote_copy(
-            src_ref=slot, dst_ref=slot, send_sem=ring_send.at[1, s], recv_sem=ring_recv.at[1, s],
-            device_id=(left, ka), device_id_type=MESH,
+            src_ref=piece,
+            dst_ref=piece,
+            send_sem=ring_send.at[way, c, s],
+            recv_sem=ring_recv.at[way, c, s],
+            device_id=(right if way == 0 else left, ka),
+            device_id_type=MESH,
         )
 
     def pair_step(i):
@@ -273,16 +273,33 @@
         )
 
     blocks = q_rows // ROWS
-    rights, lefts = n // 2, n - 1 - n // 2
-    both = min(blocks, lefts)
+    even = n % 2 == 0
+    full = n - 1 - n // 2
+    both = min(blocks, full)
+
+    for c in range(2):
+        for way in range(2):
+            hop(way, 0, c).start()
+
+    def advance(s):
+        for c in range(2):
+            for way in range(2):
+                hop(way, s, c).wait_recv()
+                if even and way == c:
+                    hop(way, s + 1, c).start()
+                else:
+
+                    @pl.when(s + 1 < full)
+                    def _():
+                        hop(way, s + 1, c).start()
 
     def with_pair(s, carry):
-        a, b = to_right(s), to_left(s)
-        a.start()
-        b.start()
         pair_step(s)
-        a.wait()
-        b.wait()
+        advance(s)
+        return carry
+
+    def only_ring(s, carry):
+        advance(s)
         return carry
 
     lax.fori_loop(0, both, with_pair, 0)
@@ -310,20 +327,19 @@
     for copy in copies:
         copy.start()
 
-    def only_ring(s, carry):
-        a, b = to_right(s), to_left(s)
-        a.start()
-        b.start()
-        a.wait()
-        b.wait()
+    if full > both:
+        lax.fori_loop(both, full, only_ring, 0)
+    if even:
+        hop(0, full, 0).wait()
+        hop(1, full, 1).wait()
+
+    def drain(s, carry):
+        for c in range(2):
+            for way in range(2):
+                hop(way, s, c).wait_send()
         return carry
 
-    if lefts > both:
-        lax.fori_loop(both, lefts, only_ring, 0)
-    for s in range(lefts, rights):
-        last = to_right(s)
-        last.start()
-        last.wait()
+    lax.fori_loop(0, full, drain, 0)
     for copy in copies:
         copy.wait()
 
@@ -350,8 +366,8 @@
             pltpu.VMEM((heads, ROWS, keys), F32),
             pltpu.VMEM((heads, q_rows, keys), BF16),
             pltpu.SemaphoreType.DMA((2,)),
-            pltpu.SemaphoreType.DMA((2, n // 2)),
-            pltpu.SemaphoreType.DMA((2, n // 2)),
+            pltpu.SemaphoreType.DMA((2, 2, n // 2)),
+            pltpu.SemaphoreType.DMA((2, 2, n // 2)),
             pltpu.SemaphoreType.DMA((size - 1,)),
             pltpu.SemaphoreType.DMA((size - 1,)),
             pltpu.SemaphoreType.DMA((10,)),

time: 66.9 us -> 62.8 us (0.939)
  Pallas kernels: 60.8 us -> 56.6 us
    pallas_call x1, Pallas kernels: 32.8 us -> 29.3 us  [pair_call(): pl.pallas_call(pair_kernel, out_shape=(jax.ShapeDtypeStruct((q_rows, keys...]
where the time goes in v4:
time: 62.8 us; the launch traced here: 62.6 us
  Pallas kernels  56.6 us (90%)
  local copies, waits for them, and re-layouts  5.1 us (8%)
  between operations  0.85 us (1%)
    pallas_call x1, Pallas kernels, pair_call(): pl.pallas_call(pair_kernel, out_shape=(jax.ShapeDtypeStruct((q_rows, keys...  29.3 us
    pallas_call x1, Pallas kernels, reduce_call(): pl.pallas_call(reduce_kernel, out_shape=jax.ShapeDtypeStruct((rows, width...  14.7 us
    pallas_call x1, Pallas kernels, gather_call(): pl.pallas_call(gather_kernel, out_shape=(jax.ShapeDtypeStruct((rows, min(...  12.6 us
    unnamed x26, local copies, waits for them, and re-layouts  4.24 us

profile of v4, /device:TPU:1, one launch (start us, length us, event | category | flops | bytes accessed | tf_op | source)
XLA Modules:
  0.0 62.6 jit_solution(9762069814317860857)
XLA Ops:
  0.6 0.8 %constant_dynamic-slice_fusion = s32[3,96]{1,0:T(4,128)S(1)} fusion(s32[3,384]{1,0:T(4,128)} %tok_ref.1, s32[]{:T(128)S(6)} %select_n.3), kind=kLoop, calls=%fused_computation | loop fusion | bytes 2308 | tf_op jit(solution)/shard_map/dynamic_slice | solution.py:507
  1.4 0.8 %copy.16.refs_9_ = bf16[128,16]{1,0:T(8,128)(2,1)S(1)} copy(bf16[128,16]{0,1:T(8,128)(2,1)} %param.22) | data formatting | bytes 8192 | tf_op args[9]
  2.2 0.1 broadcast_in_dim.2.refs_0_
  2.3 0.0 copy-start.1
  2.3 1.7 %copy.15.w_ref = bf16[4,768,192]{2,1,0:T(8,128)(2,1)S(1)} copy(bf16[4,768,192]{1,2,0:T(8,128)(2,1)} %param.24) | data formatting | bytes 2359296 | tf_op args[11]
  4.0 0.0 copy-done.1
  4.0 0.0 copy-start.2
  4.0 0.0 copy-start.3
  4.0 0.0 copy-start.4
  4.0 0.0 copy-start.5
  4.1 0.0 copy-start.6
  4.1 0.0 copy-start.7
  4.1 0.0 copy-start.8
  4.1 0.0 copy-start.9
  4.1 0.0 copy-start.10
  4.1 12.6 %shard_map.140 = (bf16[384,256]{1,0:T(8,128)(2,1)S(1)}, bf16[384,384]{1,0:T(8,128)(2,1)S(1)}, f32[384,192]{1,0:T(8,128)S(1)}) custom-call(bf16[8,48,192]{2,1,0:T(8,128)(2,1)S(1)} %copy-done.1, bf16[4,768,192]{2,1,0:T(8,128)(2,1)S(1)} %copy.15.w_ref), custom_call_target="tpu_custom_call" | custom-call | tf_op jit(solution)/shard_map/pallas_call | solution.py:193
  16.7 0.0 copy-done.2
  16.8 0.0 copy-done.3
  16.8 0.0 copy-done.4
  16.8 0.0 copy-done.5
  16.8 0.0 copy-done.6
  16.8 0.0 copy-done.7
  16.8 0.0 copy-done.8
  16.8 0.0 copy-done.9
  16.8 0.0 copy-done.10
  16.8 0.0 copy-start
  16.9 29.3 %shard_map.141 = (bf16[48,96,128]{2,1,0:T(8,128)(2,1)S(1)}, bf16[4,4,48,96]{3,2,1,0:T(8,128)(2,1)S(1)}, bf16[8,384,384]{2,1,0:T(8,128)(2,1)S(1)}) custom-call(s32[3,384]{1,0:T(4,128)S(1)} %copy-done.2, s32[3,96,128]{2,1,0:T(8,128)S(1)} %broadcast_in_dim.2.refs_0_, bf16[48,96,128]{2,1,0:T(8,128)(2,1)S(1)} %copy-done.3, bf16[139,128]{1,0:T(8,128)(2,1)S(1)} %copy-done.7, ...), custom_call_target="tpu_custom_call" | custom-call | flops 2300000000 | bytes 4000000 | tf_op jit(solution)/shard_map/pallas_call | solution.py:355
  46.2 0.0 copy-done
  46.2 14.7 %shard_map.142 = bf16[384,192]{1,0:T(8,128)(2,1)S(1)} custom-call(bf16[384,256]{1,0:T(8,128)(2,1)S(1)} %get-tuple-element.10.q_ref, bf16[8,384,384]{2,1,0:T(8,128)(2,1)S(1)} %get-tuple-element.11.kv_ref, f32[384,192]{1,0:T(8,128)S(1)} %get-tuple-element.12.gate_ref, bf16[4,4,48,96]{3,2,1,0:T(8,128)(2,1)S(1)} %get-tuple-element.13.bias_ref, ...), custom_call_target="tpu_custom_call" | custom-call | tf_op jit(solution)/shard_map/pallas_call | solution.py:470
  60.9 1.0 %copy.19 = bf16[48,96,128]{2,1,0:T(8,128)(2,1)} copy(bf16[48,96,128]{2,1,0:T(8,128)(2,1)S(1)} %get-tuple-element.16) | data formatting | bytes 2359296
  61.9 0.7 %copy.20 = bf16[8,48,192]{2,1,0:T(8,128)(2,1)} copy(bf16[8,48,192]{2,1,0:T(8,128)(2,1)S(1)} %bitcast.3) | data formatting | bytes 294912
Async XLA Ops:
  2.3 1.7 %copy-start.1 = (bf16[8,48,192]{2,1,0:T(8,128)(2,1)S(1)}, bf16[8,48,192]{2,1,0:T(8,128)(2,1)}, u32[]{:S(2)}) copy-start(bf16[8,48,192]{2,1,0:T(8,128)(2,1)} %x_ref.1) | copy-start | bytes 442372
  4.0 12.7 %copy-start.2 = (s32[3,384]{1,0:T(4,128)S(1)}, s32[3,384]{1,0:T(4,128)}, u32[]{:S(2)}) copy-start(s32[3,384]{1,0:T(4,128)} %tok_ref.1) | copy-start | bytes 13828
  4.0 12.7 %copy-start.3 = (bf16[48,96,128]{2,1,0:T(8,128)(2,1)S(1)}, bf16[48,96,128]{2,1,0:T(8,128)(2,1)}, u32[]{:S(2)}) copy-start(bf16[48,96,128]{2,1,0:T(8,128)(2,1)} %refs_1_.1) | copy-start | bytes 3538948
  4.0 12.7 %copy-start.4 = (bf16[2,128,512]{2,1,0:T(8,128)(2,1)S(1)}, bf16[2,128,512]{2,1,0:T(8,128)(2,1)}, u32[]{:S(2)}) copy-start(bf16[2,128,512]{2,1,0:T(8,128)(2,1)} %refs_6_.1) | copy-start | bytes 786436
  4.0 12.7 %copy-start.5 = (bf16[2,256,128]{2,1,0:T(8,128)(2,1)S(1)}, bf16[2,256,128]{2,1,0:T(8,128)(2,1)}, u32[]{:S(2)}) copy-start(bf16[2,256,128]{2,1,0:T(8,128)(2,1)} %refs_7_.1) | copy-start | bytes 393220
  4.1 12.7 %copy-start.6 = (bf16[256,128]{1,0:T(8,128)(2,1)S(1)}, bf16[256,128]{1,0:T(8,128)(2,1)}, u32[]{:S(2)}) copy-start(bf16[256,128]{1,0:T(8,128)(2,1)} %refs_4_.1) | copy-start | bytes 196612
  4.1 12.7 %copy-start.7 = (bf16[139,128]{1,0:T(8,128)(2,1)S(1)}, bf16[139,128]{1,0:T(8,128)(2,1)}, u32[]{:S(2)}) copy-start(bf16[139,128]{1,0:T(8,128)(2,1)} %refs_2_.1) | copy-start | bytes 106756
  4.1 12.7 %copy-start.8 = (f32[256]{0:T(256)S(1)}, f32[256]{0:T(256)}, u32[]{:S(2)}) copy-start(f32[256]{0:T(256)} %param.16) | copy-start | bytes 3076
  4.1 12.7 %copy-start.9 = (f32[2,128]{1,0:T(2,128)S(1)}, f32[2,128]{1,0:T(2,128)}, u32[]{:S(2)}) copy-start(f32[2,128]{1,0:T(2,128)} %refs_5_.1) | copy-start | bytes 3076
  4.1 12.7 %copy-start.10 = (f32[128]{0:T(128)S(1)}, f32[128]{0:T(128)}, u32[]{:S(2)}) copy-start(f32[128]{0:T(128)} %param.21) | copy-start | bytes 1540
  16.8 29.3 %copy-start = (bf16[192,768]{1,0:T(8,128)(2,1)S(1)}, bf16[192,768]{1,0:T(8,128)(2,1)}, u32[]{:S(2)}) copy-start(bf16[192,768]{1,0:T(8,128)(2,1)} %w_ref.2) | copy-start | bytes 884740
